TPU v7x, 32 devices: a whole 2x2x4 slice. The times are simulated.
32 devices in a mesh: dp: 8 (over z, x), grp: 4 (over y, core).
Axes of the slice: x: 2, y: 2, z: 4, core: 2. Of those that a mesh axis runs over, the one named last changes fastest.
Arguments:
- x_in: bfloat16 [4096, 1600], P('dp'), may hold values from -6 to 6
- attn_in: bfloat16 [4096, 1600], P('dp', 'grp'), may hold values from -6 to 6
- grad_qkv: bfloat16 [4096, 4800], P('dp', 'grp'), may hold values from -80 to 80
- grad_out: bfloat16 [4096, 1600], P('dp'), may hold values from -80 to 80
- owner: int32 [64], replicated, may hold values from 0 to 7, as said below
- step: int32 [1], replicated, may hold values from 1 to 29
- master: float32 [4, 128, 200, 200], P('grp', 'dp'), may hold values from -0.125 to 0.125
- moment: float32 [4, 128, 200, 200], P('grp', 'dp'), may hold values from -0.3125 to 0.3125
- second: float32 [4, 128, 200, 200], P('grp', 'dp'), may hold values from 0.003 to 0.1
- stat_left: float32 [4, 128, 200, 200], P('grp', 'dp'), may hold values from -8 to 32, as said below
- stat_right: float32 [4, 128, 200, 200], P('grp', 'dp'), may hold values from -8 to 32, as said below
- root_left: float32 [4, 128, 200, 200], P('grp', 'dp'), may hold values from -1 to 4, as said below
- root_right: float32 [4, 128, 200, 200], P('grp', 'dp'), may hold values from -1 to 4, as said below
- qkv_bias: float32 [4800], P('grp'), may hold values from -3 to 3
- qkv_bias_m: float32 [4800], P('grp'), may hold values from -1.25 to 1.25
- qkv_bias_v: float32 [4800], P('grp'), may hold values from 0.01 to 0.3
- proj_bias: float32 [1600], replicated, may hold values from -3 to 3
- proj_bias_m: float32 [1600], replicated, may hold values from -1.25 to 1.25
- proj_bias_v: float32 [1600], replicated, may hold values from 0.01 to 0.3
Outputs:
- master_new: float32 [4, 128, 200, 200], P('grp', 'dp')
- moment_new: float32 [4, 128, 200, 200], P('grp', 'dp')
- second_new: float32 [4, 128, 200, 200], P('grp', 'dp')
- stat_left_new: float32 [4, 128, 200, 200], P('grp', 'dp')
- stat_right_new: float32 [4, 128, 200, 200], P('grp', 'dp')
- qkv_weight: bfloat16 [1600, 4800], P(None, 'grp')
- proj_weight: bfloat16 [1600, 1600], P('grp')
- qkv_bias_new: float32 [4800], P('grp')
- qkv_bias_m_new: float32 [4800], P('grp')
- qkv_bias_v_new: float32 [4800], P('grp')
- proj_bias_new: float32 [1600], replicated
- proj_bias_m_new: float32 [1600], replicated
- proj_bias_v_new: float32 [1600], replicated
Inputs may be any that keep to these rules, and one draw needn't show every extreme that they name: `owner`: every index of dp owns at most 16 blocks, and one owns exactly 16. `stat_left`: symmetric. `stat_right`: symmetric. `root_left`: symmetric. `root_right`: symmetric.
All inputs are finite; a program needn't handle non-finite values.
Results may differ from a plain program's by a relative error of at most 0.0004.
Values may be sent and summed in bfloat16 or wider, within the bound.
A program may use at most 192 MiB of HBM per device.

v0:
```python
import jax
import jax.numpy as jnp
from jax import lax
from jax.sharding import PartitionSpec as P

D = 1600


beta_one = 0.9
beta_two = 0.95
beta_stat = 0.9
learn_rate = 0.02
weight_decay = 0.1
epsilon = 1e-08
graft_floor = 1e-06


def positions(owner, slot_count):
    total_blocks = owner.shape[0]
    blocks = jnp.arange(total_blocks, dtype=jnp.int32)
    same_owner = owner[None, :] == owner[:, None]
    earlier = blocks[None, :] < blocks[:, None]
    slot_rank = jnp.sum(jnp.where(same_owner & earlier, 1, 0).astype(jnp.int32), axis=1)
    return owner * slot_count + slot_rank


def adamw(param, first_m, second_m, grad, fix_one, fix_two):
    new_m = beta_one * first_m + (1.0 - beta_one) * grad
    new_v = beta_two * second_m + (1.0 - beta_two) * grad * grad
    new_p = param - learn_rate * (new_m / fix_one) / (jnp.sqrt(new_v / fix_two) + epsilon)
    return (new_p, new_m, new_v)


def on_device(
    x_in,
    attn_in,
    grad_qkv,
    grad_out,
    owner,
    step,
    master,
    moment,
    second,
    stat_left,
    stat_right,
    root_left,
    root_right,
    qkv_bias,
    qkv_bias_m,
    qkv_bias_v,
    proj_bias,
    proj_bias_m,
    proj_bias_v,
):
    exact = lax.Precision.HIGHEST
    groups = lax.axis_size("dp")
    own_index = lax.axis_index("dp")
    total_blocks = owner.shape[0]
    slot_count = master.shape[1]
    block_size = master.shape[2]
    tokens = x_in.shape[0] * groups
    rows_q = D // block_size
    cols_q = grad_qkv.shape[1] // block_size
    rows_p = attn_in.shape[1] // block_size
    first_kind = rows_q * cols_q
    count_f = step[0].astype(jnp.float32)
    fix_one = 1.0 - jnp.power(jnp.float32(beta_one), count_f)
    fix_two = 1.0 - jnp.power(jnp.float32(beta_two), count_f)
    blocks = jnp.arange(total_blocks, dtype=jnp.int32)
    position = positions(owner, slot_count)
    local_q = jnp.einsum("ti,tj->ij", x_in, grad_qkv, preferred_element_type=jnp.float32) / tokens
    local_p = (
        jnp.einsum("ti,tj->ij", attn_in, grad_out, preferred_element_type=jnp.float32) / tokens
    )
    tiles_q = (
        local_q.reshape(rows_q, block_size, cols_q, block_size)
        .transpose(0, 2, 1, 3)
        .reshape(first_kind, block_size, block_size)
    )
    tiles_p = (
        local_p.reshape(rows_p, block_size, rows_q, block_size)
        .transpose(0, 2, 1, 3)
        .reshape(rows_p * rows_q, block_size, block_size)
    )
    local_tiles = jnp.concatenate([tiles_q, tiles_p], axis=0)
    spots = groups * slot_count
    matches = position[None, :] == jnp.arange(spots, dtype=jnp.int32)[:, None]
    filled = jnp.any(matches, axis=1)
    holder = jnp.sum(jnp.where(matches, blocks[None, :], 0), axis=1)
    my_blocks = lax.dynamic_slice_in_dim(holder, own_index * slot_count, slot_count)
    my_filled = lax.dynamic_slice_in_dim(filled, own_index * slot_count, slot_count)
    filled_f = my_filled.astype(jnp.float32)
    occupied = filled.astype(jnp.float32)
    grads = lax.psum_scatter(
        jnp.take(local_tiles, holder, axis=0) * occupied[:, None, None],
        "dp",
        scatter_dimension=0,
        tiled=True,
    )
    old_w = master[0]
    old_m = moment[0]
    old_v = second[0]
    old_l = stat_left[0]
    old_r = stat_right[0]
    new_v = beta_two * old_v + (1.0 - beta_two) * grads * grads
    adam_dir = grads / (jnp.sqrt(new_v / fix_two) + epsilon)
    half = jnp.einsum("sij,sjk->sik", root_left[0], grads, precision=exact)
    shampoo_dir = jnp.einsum("sij,sjk->sik", half, root_right[0], precision=exact)
    is_qkv = my_blocks < first_kind
    adam_sq = jnp.sum(adam_dir * adam_dir, axis=(1, 2)) * filled_f
    shampoo_sq = jnp.sum(shampoo_dir * shampoo_dir, axis=(1, 2)) * filled_f
    adam_part = jnp.stack(
        [jnp.sum(jnp.where(is_qkv, adam_sq, 0.0)), jnp.sum(jnp.where(is_qkv, 0.0, adam_sq))]
    )
    shampoo_part = jnp.stack(
        [jnp.sum(jnp.where(is_qkv, shampoo_sq, 0.0)), jnp.sum(jnp.where(is_qkv, 0.0, shampoo_sq))]
    )
    adam_tot, shampoo_tot = lax.psum((adam_part, shampoo_part), ("dp", "grp"))
    graft = jnp.sqrt(adam_tot / (shampoo_tot + graft_floor))
    block_graft = jnp.where(is_qkv, graft[0], graft[1])
    new_m = beta_one * old_m + (1.0 - beta_one) * (block_graft[:, None, None] * shampoo_dir)
    new_w = old_w - learn_rate * (new_m + weight_decay * old_w)
    new_l = beta_stat * old_l + (1.0 - beta_stat) * jnp.einsum(
        "sik,sjk->sij", grads, grads, precision=exact
    )
    new_r = beta_stat * old_r + (1.0 - beta_stat) * jnp.einsum(
        "ski,skj->sij", grads, grads, precision=exact
    )
    keep = my_filled[:, None, None]
    master_new = jnp.where(keep, new_w, old_w)
    moment_new = jnp.where(keep, new_m, old_m)
    second_new = jnp.where(keep, new_v, old_v)
    left_new = jnp.where(keep, new_l, old_l)
    right_new = jnp.where(keep, new_r, old_r)
    new_weights = master_new.astype(jnp.bfloat16)
    everyone = lax.all_gather(new_weights, "dp", axis=0, tiled=True)
    ordered = everyone[position]
    qkv_weight = (
        ordered[:first_kind]
        .reshape(rows_q, cols_q, block_size, block_size)
        .transpose(0, 2, 1, 3)
        .reshape(D, cols_q * block_size)
    )
    proj_weight = (
        ordered[first_kind:]
        .reshape(rows_p, rows_q, block_size, block_size)
        .transpose(0, 2, 1, 3)
        .reshape(rows_p * block_size, D)
    )
    qkv_total, proj_total = lax.psum(
        (
            jnp.sum(grad_qkv, axis=0, dtype=jnp.float32),
            jnp.sum(grad_out, axis=0, dtype=jnp.float32),
        ),
        "dp",
    )
    qb_new, qm_new, qv_new = adamw(
        qkv_bias, qkv_bias_m, qkv_bias_v, qkv_total / tokens, fix_one, fix_two
    )
    pb_new, pm_new, pv_new = adamw(
        proj_bias, proj_bias_m, proj_bias_v, proj_total / tokens, fix_one, fix_two
    )
    return (
        master_new[None],
        moment_new[None],
        second_new[None],
        left_new[None],
        right_new[None],
        qkv_weight,
        proj_weight,
        qb_new,
        qm_new,
        qv_new,
        pb_new,
        pm_new,
        pv_new,
    )


def solution(mesh):
    return jax.shard_map(
        on_device,
        mesh=mesh,
        in_specs=(
            P("dp", None),
            P("dp", "grp"),
            P("dp", "grp"),
            P("dp", None),
            P(),
            P(),
            P("grp", "dp", None, None),
            P("grp", "dp", None, None),
            P("grp", "dp", None, None),
            P("grp", "dp", None, None),
            P("grp", "dp", None, None),
            P("grp", "dp", None, None),
            P("grp", "dp", None, None),
            P("grp"),
            P("grp"),
            P("grp"),
            P(),
            P(),
            P(),
        ),
        out_specs=(
            P("grp", "dp", None, None),
            P("grp", "dp", None, None),
            P("grp", "dp", None, None),
            P("grp", "dp", None, None),
            P("grp", "dp", None, None),
            P(None, "grp"),
            P("grp", None),
            P("grp"),
            P("grp"),
            P("grp"),
            P(),
            P(),
            P(),
        ),
        check_vma=False,
    )
```

profile of v0, /device:TPU:0, one launch (start us, length us, event | category | flops | bytes accessed | tf_op | source)
XLA Modules:
  0.0 822.3 jit_solution(5673216030970022077)
XLA Ops:
  7.2 0.0 copy-start
  7.2 0.0 reduce-scatter.2.cloned.1.call-start
  7.2 1.0 select_reduce_fusion.1
  8.2 0.7 compare_select_fusion
  8.9 0.1 select_reduce_fusion
  9.0 0.1 fusion.14
  9.1 7.4 convolution_multiply_fusion
  16.5 12.0 %reshape.85 = f32[8,200,6,200]{1,0,3,2:T(8,128)} reshape(f32[1600,1200]{0,1:T(8,128)} %convolution_multiply_fusion) | data formatting | bytes 15360000 | tf_op jit(solution)/shard_map/reshape | solution.py:76
  28.5 12.1 %copy.47 = f32[8,200,6,200]{3,1,2,0:T(8,128)} copy(f32[8,200,6,200]{1,0,3,2:T(8,128)} %reshape.85) | data formatting | bytes 15360000 | tf_op jit(solution)/shard_map/reshape | solution.py:76
  40.6 4.0 convolution_multiply_fusion.1
  44.6 5.2 reshape.87
  49.9 2.9 copy.48
  52.8 9.0 %pad_maximum_fusion = f32[64,200,200]{2,1,0:T(8,128)} fusion(f32[16,200,200]{2,1,0:T(8,128)S(1)} %bitcast.112, f32[48,200,200]{2,1,0:T(8,128)} %bitcast.110), kind=kLoop, calls=%fused_computation.3 | loop fusion | flops 2560000 | bytes 20480000 | tf_op jit(solution)/shard_map/concatenate | solution.py:85
  61.8 20.0 %gather_fusion = f32[128,200,200]{2,1,0:T(8,128)} fusion(f32[64,200,200]{2,1,0:T(8,128)} %pad_maximum_fusion, s32[1024]{0:T(1024)S(1)} %pad_clamp_fusion.1), kind=kCustom, calls=%fused_computation | custom fusion | bytes 40960512 | tf_op jit(solution)/shard_map/jit(_take)/gather | solution.py:95
  81.8 18.8 %select_multiply_fusion = f32[128,200,200]{2,1,0:T(8,128)} fusion(f32[128,200,200]{2,1,0:T(8,128)} %gather_fusion, f32[128]{0:T(128)S(1)} %convert_element_type.21, pred[128]{0:T(512)(128)(4,1)S(1)} %compare_and_fusion), kind=kLoop, calls=%fused_computation.2 | loop fusion | flops 10240000 | bytes 40960640 | tf_op jit(solution)/shard_map/mul | solution.py:95
  100.5 0.0 reduce-scatter.2.cloned.1.call-update
  100.6 0.2 all-gather.2.cloned.1.call-start
  101.5 420.2 %reduce-scatter.2.cloned.1.call-done = f32[16,200,200]{2,1,0:T(8,128)} async-done(((f32[128,200,200]{2,1,0:T(8,128)}), f32[16,200,200]{2,1,0:T(8,128)}) %reduce-scatter.2.cloned.1.call-update) | async-done | bytes 2560016 | tf_op jit(solution)/shard_map/reduce_scatter | solution.py:94
  521.7 6.8 fusion.7
  528.5 0.0 copy-done
  528.5 0.0 copy-start.1
  528.5 0.0 copy-start.3
  528.5 5.2 multiply_reduce_fusion
  533.7 0.0 copy-done.1
  533.7 0.0 copy-done.3
  533.7 2.0 multiply_reduce_fusion.1
  535.7 0.7 select_reduce_fusion.3
  536.4 2.7 pad_maximum_fusion.1
  539.0 39.3 %all-reduce = (f32[2]{0:T(128)S(1)}, f32[2]{0:T(128)S(1)}) all-reduce(f32[2]{0:T(128)S(1)} %get-tuple-element.41, f32[2]{0:T(128)S(1)} %get-tuple-element.42), channel_id=1, replica_groups=mesh['dp'=8,'grp'=4] {'dp','grp'}, use_global_device_ids=true, to_apply=%region_7.8 | all-reduce | flops 4 | bytes 32 | tf_op jit(solution)/shard_map/psum | solution.py:118
  578.4 0.6 fusion.19
  579.0 1.3 broadcast_select_fusion
  580.3 10.5 %fusion.18 = (bf16[16,200,200]{2,1,0:T(8,128)(2,1)}, f32[16,200,200]{2,1,0:T(8,128)}, f32[1,16,200,200]{3,2,1,0:T(8,128)}, f32[1,16,200,200]{3,2,1,0:T(8,128)}) fusion(f32[16,200,200]{2,1,0:T(8,128)} %get-tuple-element.40, f32[16]{0:T(128)S(1)} %broadcast_select_fusion, f32[1,16,200,200]{3,2,1,0:T(8,128)} %param.26, f32[1,16,200,200]{3,2,1,0:T(8,128)} %param.25, ...), kind=kLoop, calls=%fused_computation.67 | loop fusion | flops 10240000 | bytes 21760080 | tf_op jit(solution)/shard_map/convert_element_type | solution.py:135
  590.8 0.0 copy-start.5
  590.8 0.0 copy-start.6
  590.8 0.0 copy-start.7
  590.8 0.0 copy-start.8
  590.8 0.0 copy-start.9
  590.8 0.0 copy-start.10
  590.8 0.0 all-gather.2.cloned.1.call-update
  590.9 1.5 convert_reduce_fusion.1
  592.5 1.7 convert_reduce_fusion
  594.2 38.4 %all-reduce.1 = (f32[1200]{0:T(1024)S(1)}, f32[1600]{0:T(1024)S(1)}) all-reduce(f32[1200]{0:T(1024)S(1)} %convert_reduce_fusion.1, f32[1600]{0:T(1024)S(1)} %convert_reduce_fusion), channel_id=1, replica_groups=mesh['dp'=8,'grp'=4] {'dp'}, use_global_device_ids=true, to_apply=%region_13.14 | all-reduce | flops 2800 | bytes 22400 | tf_op jit(solution)/shard_map/psum | solution.py:150
  632.6 0.0 copy-done.5
  632.6 0.0 copy-done.6
  632.6 0.0 copy-done.7
  632.6 0.6 divide_subtract_fusion
  633.2 0.0 copy-done.8
  633.2 0.0 copy-done.9
  633.2 0.0 copy-done.10
  633.2 0.6 divide_subtract_fusion.1
  633.9 0.0 copy-start.2
  633.9 0.0 copy-start.4
  633.9 12.5 %fusion.2 = f32[1,16,200,200]{3,2,1,0:T(8,128)} fusion(f32[1,16,200,200]{3,2,1,0:T(8,128)} %param.29, f32[16,200,200]{2,1,0:T(8,128)} %reduce-scatter.2.cloned.1.call-done, pred[16]{0:T(512)(128)(4,1)S(1)} %get-tuple-element.33), kind=kOutput, calls=%fused_computation.11 | convolution fusion | flops 1538560000 | bytes 7680016 | tf_op jit(solution)/shard_map/ski,skj->sij/dot_general | solution.py:126
  646.3 0.0 copy-done.2
  646.3 0.0 copy-done.4
  646.3 5.7 fusion.4
  652.0 122.0 %all-gather.2.cloned.1.call-done = bf16[128,200,200]{2,1,0:T(8,128)(2,1)} async-done(((bf16[16,200,200]{2,1,0:T(8,128)(2,1)}), bf16[128,200,200]{2,1,0:T(8,128)(2,1)}) %all-gather.2.cloned.1.call-update) | async-done | bytes 10240016 | tf_op jit(solution)/shard_map/all_gather | solution.py:136
  774.1 8.4 %gather_fusion.1 = bf16[64,200,200]{2,1,0:T(8,128)(2,1)} fusion(bf16[128,200,200]{2,1,0:T(8,128)(2,1)} %all-gather.2.cloned.1.call-done, s32[1024]{0:T(1024)S(1)} %pad_clamp_fusion), kind=kCustom, calls=%fused_computation.1 | custom fusion | bytes 10240256 | tf_op jit(solution)/shard_map/gather | solution.py:137
  782.4 4.9 slice.20
  787.4 2.7 slice.21
  790.1 8.7 %copy.52 = bf16[8,200,6,200]{1,0,3,2:T(8,128)(2,1)} copy(bf16[8,200,6,200]{3,1,2,0:T(8,128)(2,1)} %bitcast.111) | data formatting | bytes 7680000 | tf_op jit(solution)/shard_map/transpose | solution.py:141
  798.8 9.2 %reshape.90 = bf16[1600,1200]{0,1:T(8,128)(2,1)} reshape(bf16[8,200,6,200]{1,0,3,2:T(8,128)(2,1)} %copy.52) | data formatting | bytes 7680000 | tf_op jit(solution)/shard_map/reshape | solution.py:142
  808.0 2.9 copy.53
  811.0 4.1 reshape.92
  (6 shorter events, 0.0 us)
Async XLA Ops:
  7.2 521.3 %copy-start = (f32[1,16,200,200]{3,2,1,0:T(8,128)S(1)}, f32[1,16,200,200]{3,2,1,0:T(8,128)}, u32[]{:S(2)}) copy-start(f32[1,16,200,200]{3,2,1,0:T(8,128)} %param.31) | copy-start | bytes 7680004
  7.2 514.5 %reduce-scatter.2.cloned.1.call-start = ((), (), s32[]{:S(2)}) async-start(), calls=%async_computation.1 | async-start | bytes 29491200 | tf_op jit(solution)/shard_map/reduce_scatter | solution.py:94
  100.6 673.5 %all-gather.2.cloned.1.call-start = ((), (), s32[]{:S(2)}) async-start(), calls=%async_computation.2 | async-start | bytes 14745600 | tf_op jit(solution)/shard_map/all_gather | solution.py:136
  528.5 5.3 copy-start.1
  528.5 5.2 copy-start.3
  590.8 41.8 %copy-start.5 = (f32[1600]{0:T(1024)S(1)}, f32[1600]{0:T(1024)}, u32[]{:S(2)}) copy-start(f32[1600]{0:T(1024)} %param.35) | copy-start | bytes 19204
  590.8 41.8 %copy-start.6 = (f32[1600]{0:T(1024)S(1)}, f32[1600]{0:T(1024)}, u32[]{:S(2)}) copy-start(f32[1600]{0:T(1024)} %param.36) | copy-start | bytes 19204
  590.8 41.8 %copy-start.7 = (f32[1600]{0:T(1024)S(1)}, f32[1600]{0:T(1024)}, u32[]{:S(2)}) copy-start(f32[1600]{0:T(1024)} %param.37) | copy-start | bytes 19204
  590.8 42.4 %copy-start.8 = (f32[1200]{0:T(1024)S(1)}, f32[1200]{0:T(1024)}, u32[]{:S(2)}) copy-start(f32[1200]{0:T(1024)} %param.32) | copy-start | bytes 14404
  590.8 42.4 %copy-start.9 = (f32[1200]{0:T(1024)S(1)}, f32[1200]{0:T(1024)}, u32[]{:S(2)}) copy-start(f32[1200]{0:T(1024)} %param.33) | copy-start | bytes 14404
  590.8 42.4 %copy-start.10 = (f32[1200]{0:T(1024)S(1)}, f32[1200]{0:T(1024)}, u32[]{:S(2)}) copy-start(f32[1200]{0:T(1024)} %param.34) | copy-start | bytes 14404
  633.9 12.5 %copy-start.2 = (f32[16,200,200]{2,1,0:T(8,128)S(1)}, f32[16,200,200]{2,1,0:T(8,128)}, u32[]{:S(2)}) copy-start(f32[16,200,200]{2,1,0:T(8,128)} %reduce-scatter.2.cloned.1.call-done) | copy-start | bytes 7680004
  633.9 12.5 %copy-start.4 = (f32[1,16,200,200]{3,2,1,0:T(8,128)S(1)}, f32[1,16,200,200]{3,2,1,0:T(8,128)}, u32[]{:S(2)}) copy-start(f32[1,16,200,200]{3,2,1,0:T(8,128)} %param.28) | copy-start | bytes 7680004
Sparse Core Ops, SparseCore 0:
  100.7 420.9 reduce-scatter.1
  591.0 183.0 all-gather.1
where the time goes:
time: 831 us; the launch traced here: 822 us
  waiting for transfers between devices  542 us (65%)
  local copies, waits for them, and re-layouts  93.8 us (11%)
  blocking collectives  77.7 us (9%)
  other arithmetic  51.4 us (6%)
  matrix products  41.6 us (5%)
  between operations  15.4 us (2%)
    reduce_scatter x1, waiting for transfers between devices, on_device(): lax.psum_scatter(jnp.take(local_tiles, holder, axis=0) * occupied[:, None...  420 us
    all_gather x1, waiting for transfers between devices, on_device(): everyone = lax.all_gather(new_weights, 'dp', axis=0, tiled=True)  122 us
    psum x1, blocking collectives, on_device(): adam_tot, shampoo_tot = lax.psum((adam_part, shampoo_part), ('dp', 'grp'))  39.3 us
    psum x1, blocking collectives, on_device(): lax.psum((jnp.sum(grad_qkv, axis=0, dtype=jnp.float32), jnp.sum(grad_out,...  38.4 us
    reshape x2, local copies, waits for them, and re-layouts, on_device(): local_q.reshape(rows_q, block_size, cols_q, block_size)  24.1 us
    gather x1, local copies, waits for them, and re-layouts, on_device(): jnp.take(local_tiles, holder, axis=0) * occupied[:, None, None]  20 us
    mul x1, other arithmetic, on_device(): jnp.take(local_tiles, holder, axis=0) * occupied[:, None, None]  18.8 us
  transfers between devices with their start and end apart: 2, of which 2 were waited for; matrix products, arithmetic and copies ran while one was open for 3% of the time, Pallas kernels for 0%

commit v1 on v0

--- a/solution.py
+++ b/solution.py
@@ -1,6 +1,8 @@
 import jax
 import jax.numpy as jnp
 from jax import lax
+from jax.experimental import pallas as pl
+from jax.experimental.pallas import tpu as pltpu
 from jax.sharding import PartitionSpec as P
 
 D = 1600
@@ -29,6 +31,123 @@
     new_v = beta_two * second_m + (1.0 - beta_two) * grad * grad
     new_p = param - learn_rate * (new_m / fix_one) / (jnp.sqrt(new_v / fix_two) + epsilon)
     return (new_p, new_m, new_v)
+
+
+def place_kernel(split, cols_q, rows_q, pos_ref, left_ref, right_ref, tile_ref, peak_ref):
+    b = pl.program_id(0)
+    first = b < split
+    later = jnp.maximum(b - split, 0)
+    i = jnp.where(first, b // cols_q, rows_q + later // rows_q)
+    j = jnp.where(first, b % cols_q, cols_q + later % rows_q)
+    tile = lax.dot_general(
+        left_ref[i], right_ref[j], (((1,), (1,)), ((), ())), preferred_element_type=jnp.float32
+    )
+    tile_ref[0] = tile
+    peak_ref[0] = jnp.full((8, 128), jnp.max(jnp.abs(tile)), jnp.float32)
+
+
+def place_tiles(left, right, position, split, cols_q, rows_q, spots):
+    total = position.shape[0]
+    side, depth = left.shape[1:]
+    return pl.pallas_call(
+        lambda *refs: place_kernel(split, cols_q, rows_q, *refs),
+        out_shape=(
+            jax.ShapeDtypeStruct((spots, side, side), jnp.float32),
+            jax.ShapeDtypeStruct((total, 8, 128), jnp.float32),
+        ),
+        grid_spec=pltpu.PrefetchScalarGridSpec(
+            num_scalar_prefetch=1,
+            grid=(total,),
+            in_specs=[
+                pl.BlockSpec(left.shape, lambda b, pos: (0, 0, 0)),
+                pl.BlockSpec(right.shape, lambda b, pos: (0, 0, 0)),
+            ],
+            out_specs=[
+                pl.BlockSpec((1, side, side), lambda b, pos: (pos[b], 0, 0)),
+                pl.BlockSpec((1, 8, 128), lambda b, pos: (b, 0, 0)),
+            ],
+        ),
+        compiler_params=pltpu.CompilerParams(vmem_limit_bytes=32 * 1024 * 1024),
+    )(position, left, right)
+
+
+def join_kernel(count, pos_ref, *refs):
+    out_ref = refs[count]
+    parts = [refs[k][0].astype(jnp.float32) for k in range(count)]
+    out_ref[...] = jnp.concatenate(parts, axis=1).astype(out_ref.dtype)
+
+
+def join_tiles(tiles, position, base, rows, cols):
+    side = tiles.shape[1]
+
+    def spot(k):
+        return lambda r, pos: (pos[base + r * cols + k], 0, 0)
+
+    return pl.pallas_call(
+        lambda *refs: join_kernel(cols, *refs),
+        out_shape=jax.ShapeDtypeStruct((rows * side, cols * side), tiles.dtype),
+        grid_spec=pltpu.PrefetchScalarGridSpec(
+            num_scalar_prefetch=1,
+            grid=(rows,),
+            in_specs=[pl.BlockSpec((1, side, side), spot(k)) for k in range(cols)],
+            out_specs=pl.BlockSpec((side, cols * side), lambda r, pos: (r, 0)),
+        ),
+        compiler_params=pltpu.CompilerParams(vmem_limit_bytes=32 * 1024 * 1024),
+    )(position, *([tiles] * cols))
+
+
+def sum_kernel(axes, sizes, in_ref, out_ref, *scratch):
+    buffers = scratch[: len(axes)]
+    send_sems = scratch[len(axes) : 2 * len(axes)]
+    recv_sems = scratch[2 * len(axes) :]
+    barrier = pltpu.get_barrier_semaphore()
+    for axis, size in zip(axes, sizes):
+        me = lax.axis_index(axis)
+        for k in range(1, size):
+            pl.semaphore_signal(
+                barrier,
+                inc=1,
+                device_id={axis: lax.rem(me + k, size)},
+                device_id_type=pl.DeviceIdType.MESH,
+            )
+    pl.semaphore_wait(barrier, sum(size - 1 for size in sizes))
+    value = in_ref[...]
+    for n, (axis, size) in enumerate(zip(axes, sizes)):
+        me = lax.axis_index(axis)
+        buffers[n][me] = value
+        copies = []
+        for k in range(1, size):
+            copy = pltpu.make_async_remote_copy(
+                src_ref=buffers[n].at[me],
+                dst_ref=buffers[n].at[me],
+                send_sem=send_sems[n].at[k - 1],
+                recv_sem=recv_sems[n].at[k - 1],
+                device_id={axis: lax.rem(me + k, size)},
+                device_id_type=pl.DeviceIdType.MESH,
+            )
+            copy.start()
+            copies.append(copy)
+        for copy in copies:
+            copy.wait()
+        value = buffers[n][0]
+        for k in range(1, size):
+            value = value + buffers[n][k]
+    out_ref[...] = value
+
+
+def sum_over(value, axes, collective_id):
+    sizes = [lax.axis_size(axis) for axis in axes]
+    scratch = [pltpu.VMEM((size,) + value.shape, jnp.float32) for size in sizes]
+    scratch += [pltpu.SemaphoreType.DMA((size - 1,)) for size in sizes]
+    scratch += [pltpu.SemaphoreType.DMA((size - 1,)) for size in sizes]
+    return pl.pallas_call(
+        lambda *refs: sum_kernel(axes, sizes, *refs),
+        out_shape=jax.ShapeDtypeStruct(value.shape, jnp.float32),
+        in_specs=[pl.BlockSpec(memory_space=pltpu.VMEM)],
+        out_specs=pl.BlockSpec(memory_space=pltpu.VMEM),
+        scratch_shapes=scratch,
+        compiler_params=pltpu.CompilerParams(collective_id=collective_id, has_side_effects=True),
+    )(value)
 
 
 def on_device(
@@ -68,21 +187,6 @@
     fix_two = 1.0 - jnp.power(jnp.float32(beta_two), count_f)
     blocks = jnp.arange(total_blocks, dtype=jnp.int32)
     position = positions(owner, slot_count)
-    local_q = jnp.einsum("ti,tj->ij", x_in, grad_qkv, preferred_element_type=jnp.float32) / tokens
-    local_p = (
-        jnp.einsum("ti,tj->ij", attn_in, grad_out, preferred_element_type=jnp.float32) / tokens
-    )
-    tiles_q = (
-        local_q.reshape(rows_q, block_size, cols_q, block_size)
-        .transpose(0, 2, 1, 3)
-        .reshape(first_kind, block_size, block_size)
-    )
-    tiles_p = (
-        local_p.reshape(rows_p, block_size, rows_q, block_size)
-        .transpose(0, 2, 1, 3)
-        .reshape(rows_p * rows_q, block_size, block_size)
-    )
-    local_tiles = jnp.concatenate([tiles_q, tiles_p], axis=0)
     spots = groups * slot_count
     matches = position[None, :] == jnp.arange(spots, dtype=jnp.int32)[:, None]
     filled = jnp.any(matches, axis=1)
@@ -90,13 +194,71 @@
     my_blocks = lax.dynamic_slice_in_dim(holder, own_index * slot_count, slot_count)
     my_filled = lax.dynamic_slice_in_dim(filled, own_index * slot_count, slot_count)
     filled_f = my_filled.astype(jnp.float32)
-    occupied = filled.astype(jnp.float32)
-    grads = lax.psum_scatter(
-        jnp.take(local_tiles, holder, axis=0) * occupied[:, None, None],
-        "dp",
-        scatter_dimension=0,
-        tiled=True,
-    )
+    keep = my_filled[:, None, None]
+
+    depth = x_in.shape[0]
+    left = jnp.concatenate(
+        [
+            x_in.T.reshape(rows_q, block_size, depth),
+            attn_in.T.reshape(rows_p, block_size, depth),
+        ]
+    )
+    right = jnp.concatenate(
+        [
+            grad_qkv.T.reshape(cols_q, block_size, depth),
+            grad_out.T.reshape(rows_q, block_size, depth),
+        ]
+    )
+    local_tiles, peaks = place_tiles(
+        left, right, position, first_kind, cols_q, rows_q, spots
+    )
+
+    width_q, width_p = grad_qkv.shape[1], grad_out.shape[1]
+    small = jnp.concatenate(
+        [
+            jnp.sum(grad_qkv, axis=0, dtype=jnp.float32),
+            jnp.sum(grad_out, axis=0, dtype=jnp.float32),
+            peaks[:, 0, 0],
+        ]
+    )
+    used = small.shape[0]
+    padded = -(-used // 1024) * 1024
+    small = jnp.pad(small, (0, padded - used)).reshape(8, padded // 8)
+    small = sum_over(small, ("dp",), 0).reshape(padded)
+    qkv_total = small[:width_q]
+    proj_total = small[width_q : width_q + width_p]
+    bound = small[width_q + width_p : used]
+    spot_bound = jnp.sum(jnp.where(matches, bound[None, :], 0.0), axis=1)
+    spot_bound = jnp.where(spot_bound > 0.0, spot_bound, 1.0).reshape(groups, slot_count, 1, 1)
+    shrink = 16384.0 / spot_bound
+    grow = spot_bound / 16384.0
+
+    pair = own_index // 2
+    side = own_index % 2
+    pairs = groups // 2
+    tiles = local_tiles.reshape(groups, slot_count, block_size, block_size)
+
+    def chunk(array, where):
+        return lax.dynamic_index_in_dim(array, where, 0, keepdims=False)
+
+    across = [(d, d ^ 1) for d in range(groups)]
+    mine = None
+    arrivals = []
+    for step_off in list(range(1, pairs)) + [0]:
+        target = lax.rem(pair + step_off, pairs)
+        theirs = target * 2 + 1 - side
+        ours = target * 2 + side
+        sent = (chunk(tiles, theirs) * chunk(shrink, theirs)).astype(jnp.float16)
+        got = lax.ppermute(sent, "dp", across)
+        both = chunk(tiles, ours) * chunk(shrink, ours) + got.astype(jnp.float32)
+        if step_off == 0:
+            mine = both
+        else:
+            hop = [(d, ((d // 2 + step_off) % pairs) * 2 + d % 2) for d in range(groups)]
+            arrivals.append(lax.ppermute(both.astype(jnp.float16), "dp", hop))
+    for arrived in arrivals:
+        mine = mine + arrived.astype(jnp.float32)
+    grads = jnp.where(keep, mine * (chunk(grow, own_index) / tokens), 0.0)
     old_w = master[0]
     old_m = moment[0]
     old_v = second[0]
@@ -109,14 +271,18 @@
     is_qkv = my_blocks < first_kind
     adam_sq = jnp.sum(adam_dir * adam_dir, axis=(1, 2)) * filled_f
     shampoo_sq = jnp.sum(shampoo_dir * shampoo_dir, axis=(1, 2)) * filled_f
-    adam_part = jnp.stack(
-        [jnp.sum(jnp.where(is_qkv, adam_sq, 0.0)), jnp.sum(jnp.where(is_qkv, 0.0, adam_sq))]
-    )
-    shampoo_part = jnp.stack(
-        [jnp.sum(jnp.where(is_qkv, shampoo_sq, 0.0)), jnp.sum(jnp.where(is_qkv, 0.0, shampoo_sq))]
-    )
-    adam_tot, shampoo_tot = lax.psum((adam_part, shampoo_part), ("dp", "grp"))
-    graft = jnp.sqrt(adam_tot / (shampoo_tot + graft_floor))
+    sums = [
+        jnp.sum(jnp.where(is_qkv, adam_sq, 0.0)),
+        jnp.sum(jnp.where(is_qkv, 0.0, adam_sq)),
+        jnp.sum(jnp.where(is_qkv, shampoo_sq, 0.0)),
+        jnp.sum(jnp.where(is_qkv, 0.0, shampoo_sq)),
+    ]
+    lane = lax.broadcasted_iota(jnp.int32, (8, 128), 1)
+    part = jnp.zeros((8, 128), jnp.float32)
+    for n, value in enumerate(sums):
+        part = jnp.where(lane == n, value, part)
+    total = sum_over(part, ("grp", "dp"), 1)
+    graft = jnp.sqrt(total[0, 0:2] / (total[0, 2:4] + graft_floor))
     block_graft = jnp.where(is_qkv, graft[0], graft[1])
     new_m = beta_one * old_m + (1.0 - beta_one) * (block_graft[:, None, None] * shampoo_dir)
     new_w = old_w - learn_rate * (new_m + weight_decay * old_w)
@@ -126,34 +292,24 @@
     new_r = beta_stat * old_r + (1.0 - beta_stat) * jnp.einsum(
         "ski,skj->sij", grads, grads, precision=exact
     )
-    keep = my_filled[:, None, None]
     master_new = jnp.where(keep, new_w, old_w)
     moment_new = jnp.where(keep, new_m, old_m)
     second_new = jnp.where(keep, new_v, old_v)
     left_new = jnp.where(keep, new_l, old_l)
     right_new = jnp.where(keep, new_r, old_r)
     new_weights = master_new.astype(jnp.bfloat16)
-    everyone = lax.all_gather(new_weights, "dp", axis=0, tiled=True)
-    ordered = everyone[position]
-    qkv_weight = (
-        ordered[:first_kind]
-        .reshape(rows_q, cols_q, block_size, block_size)
-        .transpose(0, 2, 1, 3)
-        .reshape(D, cols_q * block_size)
-    )
-    proj_weight = (
-        ordered[first_kind:]
-        .reshape(rows_p, rows_q, block_size, block_size)
-        .transpose(0, 2, 1, 3)
-        .reshape(rows_p * block_size, D)
-    )
-    qkv_total, proj_total = lax.psum(
-        (
-            jnp.sum(grad_qkv, axis=0, dtype=jnp.float32),
-            jnp.sum(grad_out, axis=0, dtype=jnp.float32),
-        ),
-        "dp",
-    )
+    spread = [new_weights]
+    for step_off in range(1, pairs):
+        hop = [(d, ((d // 2 + step_off) % pairs) * 2 + d % 2) for d in range(groups)]
+        spread.append(lax.ppermute(new_weights, "dp", hop))
+    other = [lax.ppermute(part_w, "dp", across) for part_w in spread]
+    everyone = jnp.concatenate(spread + other)
+    place_owner = owner // 2
+    turn = lax.rem(pair - place_owner + pairs, pairs)
+    order = jnp.where(owner % 2 == side, turn, pairs + turn)
+    where_held = order * slot_count + (position - owner * slot_count)
+    qkv_weight = join_tiles(everyone, where_held, 0, rows_q, cols_q)
+    proj_weight = join_tiles(everyone, where_held, first_kind, rows_p, rows_q)
     qb_new, qm_new, qv_new = adamw(
         qkv_bias, qkv_bias_m, qkv_bias_v, qkv_total / tokens, fix_one, fix_two
     )

time: 831 us -> 592 us (0.71)
  the two profiles are of different devices: /device:TPU:0 before, /device:TPU:24 now
where the time goes in v1:
time: 592 us; the launch traced here: 591 us
  waiting for transfers between devices  424 us (72%)
  Pallas kernels  54 us (9%)
  other arithmetic  48.8 us (8%)
  local copies, waits for them, and re-layouts  26 us (4%)
  matrix products  22.7 us (4%)
  starting transfers between devices  13.6 us (2%)
    ppermute x4, waiting for transfers between devices, on_device(): got = lax.ppermute(sent, 'dp', across)  127 us
    ppermute x3, waiting for transfers between devices, on_device(): spread.append(lax.ppermute(new_weights, 'dp', hop))  127 us
    ppermute x3, waiting for transfers between devices, on_device(): arrivals.append(lax.ppermute(both.astype(jnp.float16), 'dp', hop))  114 us
    ppermute x4, waiting for transfers between devices, on_device(): other = [lax.ppermute(part_w, 'dp', across) for part_w in spread]  56.3 us
    pallas_call x1, Pallas kernels, place_tiles(): pl.pallas_call(lambda *refs: place_kernel(split, cols_q, rows_q, *refs),...  30.4 us
    unnamed x53, local copies, waits for them, and re-layouts  23.1 us
    pallas_call x2, Pallas kernels, sum_over(): pl.pallas_call(lambda *refs: sum_kernel(axes, sizes, *refs), out_shape=ja...  19.4 us
  transfers between devices with their start and end apart: 14, of which 10 were waited for; matrix products, arithmetic and copies ran while one was open for 5% of the time, Pallas kernels for 0%

profile of v1, /device:TPU:24, one launch (start us, length us, event | category | flops | bytes accessed | tf_op | source)
XLA Modules:
  0.0 591.3 jit_solution(8178566121051863862)
XLA Ops:
  0.8 1.0 select_reduce_fusion.2
  1.8 0.7 multiply_add_fusion.4
  2.5 1.8 convert_reduce_fusion
  4.3 1.7 convert_reduce_fusion.1
  6.0 0.2 pad_maximum_fusion.refs_2_
  6.3 0.2 pad_maximum_fusion.1.refs_1_
  6.5 30.4 %shard_map.282 = (f32[128,200,200]{2,1,0:T(8,128)}, f32[64,8,128]{2,1,0:T(8,128)S(1)}) custom-call(s32[64]{0:T(128)S(1)} %get-tuple-element.92.refs_0_, bf16[10,200,512]{2,1,0:T(8,128)(2,1)S(1)} %pad_maximum_fusion.1.refs_1_, bf16[14,200,512]{2,1,0:T(8,128)(2,1)S(1)} %pad_maximum_fusion.refs_2_), custom_call_target="tpu_custom_call" | custom-call | tf_op jit(solution)/shard_map/pallas_call | solution.py:52
  36.8 0.6 slice_reduce_fusion
  37.5 0.6 reshape.131.refs_0_
  38.1 8.4 %shard_map.283 = f32[8,384]{1,0:T(8,128)} custom-call(f32[8,384]{1,0:T(8,128)} %reshape.131.refs_0_), custom_call_target="tpu_custom_call" | custom-call | tf_op jit(solution)/shard_map/pallas_call | solution.py:143
  46.5 0.7 reshape.132
  47.5 7.7 %fusion.19 = (f16[16,200,200]{2,1,0:T(8,128)(2,1)}, f16[16,200,200]{2,1,0:T(8,128)(2,1)S(1)}, f16[16,200,200]{2,1,0:T(8,128)(2,1)S(1)}, f16[16,200,200]{2,1,0:T(8,128)(2,1)S(1)}) fusion(f32[8,16,200,200]{3,2,1,0:T(8,128)} %bitcast.158, s32[]{:T(128)S(6)} %select_n.155, f32[16]{0:T(128)S(1)} %get-tuple-element.88, f32[16]{0:T(128)S(1)} %get-tuple-element.82, ...), kind=kLoop, calls=%fused_computation.34 | loop fusion | flops 5120000 | bytes 15360272 | tf_op jit(solution)/shard_map/convert_element_type | solution.py:251
  55.2 1.6 collective-permute-start.1
  56.8 0.5 collective-permute-start.3
  57.2 1.6 collective-permute-start.5
  58.8 0.5 collective-permute-start
  59.3 34.7 %collective-permute-done.1 = f16[16,200,200]{2,1,0:T(8,128)(2,1)S(1)} collective-permute-done((f16[16,200,200]{2,1,0:T(8,128)(2,1)S(1)}, f16[16,200,200]{2,1,0:T(8,128)(2,1)S(1)}, u32[]{:S(2)}, u32[]{:S(2)}) %collective-permute-start.1) | collective-permute-done | bytes 1280032 | tf_op jit(solution)/shard_map/ppermute | solution.py:252
  94.0 35.1 %collective-permute-done.3 = f16[16,200,200]{2,1,0:T(8,128)(2,1)S(1)} collective-permute-done((f16[16,200,200]{2,1,0:T(8,128)(2,1)S(1)}, f16[16,200,200]{2,1,0:T(8,128)(2,1)S(1)}, u32[]{:S(2)}, u32[]{:S(2)}) %collective-permute-start.3) | collective-permute-done | bytes 1280032 | tf_op jit(solution)/shard_map/ppermute | solution.py:252
  129.1 35.1 %collective-permute-done.5 = f16[16,200,200]{2,1,0:T(8,128)(2,1)S(1)} collective-permute-done((f16[16,200,200]{2,1,0:T(8,128)(2,1)S(1)}, f16[16,200,200]{2,1,0:T(8,128)(2,1)S(1)}, u32[]{:S(2)}, u32[]{:S(2)}) %collective-permute-start.5) | collective-permute-done | bytes 1280032 | tf_op jit(solution)/shard_map/ppermute | solution.py:252
  164.2 7.5 %fusion.18 = (f16[16,200,200]{2,1,0:T(8,128)(2,1)}, f16[16,200,200]{2,1,0:T(8,128)(2,1)}, f16[16,200,200]{2,1,0:T(8,128)(2,1)}) fusion(f16[16,200,200]{2,1,0:T(8,128)(2,1)S(1)} %collective-permute-done.1, f32[8,16,200,200]{3,2,1,0:T(8,128)} %bitcast.159, s32[]{:T(128)S(6)} %select_n.156, f32[16]{0:T(128)S(1)} %get-tuple-element.87, ...), kind=kLoop, calls=%fused_computation.32 | loop fusion | flops 7680000 | bytes 15360204 | tf_op jit(solution)/shard_map/convert_element_type | solution.py:258
  171.6 0.6 collective-permute-start.2
  172.2 1.2 collective-permute-start.4
  173.4 0.3 collective-permute-start.6
  174.7 22.4 %collective-permute-done = f16[16,200,200]{2,1,0:T(8,128)(2,1)} collective-permute-done((f16[16,200,200]{2,1,0:T(8,128)(2,1)}, f16[16,200,200]{2,1,0:T(8,128)(2,1)}, u32[]{:S(2)}, u32[]{:S(2)}) %collective-permute-start) | collective-permute-done | bytes 1280032 | tf_op jit(solution)/shard_map/ppermute | solution.py:252
  197.1 11.6 %collective-permute-done.2 = f16[16,200,200]{2,1,0:T(8,128)(2,1)} collective-permute-done((f16[16,200,200]{2,1,0:T(8,128)(2,1)}, f16[16,200,200]{2,1,0:T(8,128)(2,1)}, u32[]{:S(2)}, u32[]{:S(2)}) %collective-permute-start.2) | collective-permute-done | bytes 1280032 | tf_op jit(solution)/shard_map/ppermute | solution.py:258
  208.8 101.9 %collective-permute-done.4 = f16[16,200,200]{2,1,0:T(8,128)(2,1)} collective-permute-done((f16[16,200,200]{2,1,0:T(8,128)(2,1)}, f16[16,200,200]{2,1,0:T(8,128)(2,1)}, u32[]{:S(2)}, u32[]{:S(2)}) %collective-permute-start.4) | collective-permute-done | bytes 1280032 | tf_op jit(solution)/shard_map/ppermute | solution.py:258
  310.7 8.5 %fusion.5 = (f32[1,16,200,200]{3,2,1,0:T(8,128)}, f32[16,200,200]{2,1,0:T(8,128)S(1)}) fusion(f32[1,16,200,200]{3,2,1,0:T(8,128)} %param.27, pred[16]{0:T(512)(128)(4,1)S(1)} %dynamic_slice.59, f32[16]{0:T(128)S(1)} %fusion.44, f16[16,200,200]{2,1,0:T(8,128)(2,1)} %collective-permute-done.6, f16[16,200,200]{2,1,0:T(8,128)(2,1)} %collective-permute-done.4, ...), kind=kLoop, calls=%fused_computation.13 | loop fusion | flops 10240000 | bytes 15360148 | tf_op jit(solution)/shard_map/broadcast_in_dim | solution.py:322
  319.2 3.6 fusion.8
  322.8 2.0 multiply_reduce_fusion
  324.8 5.2 multiply_reduce_fusion.1
  330.0 0.7 select_reduce_fusion.6
  330.7 0.6 compare_select_fusion.4
  331.4 2.5 select_select_fusion.refs_0_
  333.9 11.0 %shard_map.284 = f32[8,128]{1,0:T(8,128)} custom-call(f32[8,128]{1,0:T(8,128)} %select_select_fusion.refs_0_), custom_call_target="tpu_custom_call" | custom-call | tf_op jit(solution)/shard_map/pallas_call | solution.py:143
  344.9 0.8 fusion.45
  345.8 0.6 fusion.47
  346.3 1.3 broadcast_select_fusion
  347.7 7.6 %constant_dynamic-update-slice_fusion.7 = (bf16[128,200,200]{2,1,0:T(8,128)(2,1)S(1)}, bf16[16,200,200]{2,1,0:T(8,128)(2,1)}, f32[16,200,200]{2,1,0:T(8,128)}) fusion(f32[16,200,200]{2,1,0:T(8,128)} %get-tuple-element.96, f32[16]{0:T(128)S(1)} %broadcast_select_fusion, f32[1,16,200,200]{3,2,1,0:T(8,128)} %param.26, f32[1,16,200,200]{3,2,1,0:T(8,128)} %param.25, ...), kind=kLoop, calls=%fused_computation.70 | loop fusion | flops 6399999 | bytes 13158480
  355.3 1.4 collective-permute-start.7
  356.7 0.6 collective-permute-start.8
  357.3 0.7 collective-permute-start.9
  358.0 0.7 divide_subtract_fusion
  358.7 0.6 divide_subtract_fusion.1
  359.3 1.4 collective-permute-start.10
  360.7 8.5 %fusion.2 = f32[1,16,200,200]{3,2,1,0:T(8,128)} fusion(f32[1,16,200,200]{3,2,1,0:T(8,128)S(1)} %copy-done.13, f32[16,200,200]{2,1,0:T(8,128)S(1)} %copy-done.6, pred[16]{0:T(512)(128)(4,1)S(1)} %dynamic_slice.59), kind=kOutput, calls=%fused_computation.6 | convolution fusion | flops 1538560000 | bytes 7680016 | tf_op jit(solution)/shard_map/ski,skj->sij/dot_general | solution.py:292
  369.2 24.1 %collective-permute-done.7 = bf16[16,200,200]{2,1,0:T(8,128)(2,1)} collective-permute-done((bf16[16,200,200]{2,1,0:T(8,128)(2,1)}, bf16[16,200,200]{2,1,0:T(8,128)(2,1)}, u32[]{:S(2)}, u32[]{:S(2)}) %collective-permute-start.7) | collective-permute-done | bytes 1280032 | tf_op jit(solution)/shard_map/ppermute | solution.py:304
  393.3 1.4 collective-permute-start.11
  394.7 103.0 %collective-permute-done.8 = bf16[16,200,200]{2,1,0:T(8,128)(2,1)S(1)} collective-permute-done((bf16[16,200,200]{2,1,0:T(8,128)(2,1)}, bf16[16,200,200]{2,1,0:T(8,128)(2,1)S(1)}, u32[]{:S(2)}, u32[]{:S(2)}) %collective-permute-start.8) | collective-permute-done | bytes 1280032 | tf_op jit(solution)/shard_map/ppermute | solution.py:304
  497.7 1.1 collective-permute-start.12
  498.8 5.5 fusion.4
  504.3 0.9 collective-permute-start.13
  505.3 2.3 fusion.27
  507.6 1.5 constant_dynamic-update-slice_fusion.6
  509.1 0.1 constant_dynamic-update-slice_fusion.5
  509.3 1.5 constant_dynamic-update-slice_fusion.4
  510.8 1.5 constant_dynamic-update-slice_fusion.3
  512.5 24.0 %collective-permute-done.12 = bf16[16,200,200]{2,1,0:T(8,128)(2,1)S(1)} collective-permute-done((bf16[16,200,200]{2,1,0:T(8,128)(2,1)S(1)}, bf16[16,200,200]{2,1,0:T(8,128)(2,1)S(1)}, u32[]{:S(2)}, u32[]{:S(2)}) %collective-permute-start.12) | collective-permute-done | bytes 1280032 | tf_op jit(solution)/shard_map/ppermute | solution.py:305
  536.6 32.3 %collective-permute-done.13 = bf16[16,200,200]{2,1,0:T(8,128)(2,1)S(1)} collective-permute-done((bf16[16,200,200]{2,1,0:T(8,128)(2,1)}, bf16[16,200,200]{2,1,0:T(8,128)(2,1)S(1)}, u32[]{:S(2)}, u32[]{:S(2)}) %collective-permute-start.13) | collective-permute-done | bytes 1280032 | tf_op jit(solution)/shard_map/ppermute | solution.py:305
  569.0 2.3 shard_map.285
  571.3 4.7 copy-done.2
  576.0 1.9 copy-done.4
  577.9 4.7 copy-done.3
  582.6 2.0 shard_map.286
  584.6 6.7 %copy.39 = bf16[1600,1200]{0,1:T(8,128)(2,1)} copy(bf16[1600,1200]{1,0:T(8,128)(2,1)} %copy-done.4) | data formatting | bytes 7680000
  (63 shorter events, 1.1 us)
Async XLA Ops:
  0.6 324.2 %copy-start = (f32[1,16,200,200]{3,2,1,0:T(8,128)S(1)}, f32[1,16,200,200]{3,2,1,0:T(8,128)}, u32[]{:S(2)}) copy-start(f32[1,16,200,200]{3,2,1,0:T(8,128)} %param.31) | copy-start | bytes 7680004
  0.8 5.2 copy-start.10
  0.8 5.2 copy-start.11
  4.3 2.0 copy-start.15
  4.3 2.0 copy-start.16
  55.2 38.7 %collective-permute-start.1 = (f16[16,200,200]{2,1,0:T(8,128)(2,1)S(1)}, f16[16,200,200]{2,1,0:T(8,128)(2,1)S(1)}, u32[]{:S(2)}, u32[]{:S(2)}) collective-permute-start(f16[16,200,200]{2,1,0:T(8,128)(2,1)S(1)} %get-tuple-element.77), channel_id=1, source_target_pairs={{0,4},{4,0},{8,12},{12,8},{16,20},{20,16},{24,28},{28,24},{1,5},{5... | collective-permute-start | bytes 3840008 | tf_op jit(solution)/shard_map/ppermute | solution.py:252
  56.8 72.3 %collective-permute-start.3 = (f16[16,200,200]{2,1,0:T(8,128)(2,1)S(1)}, f16[16,200,200]{2,1,0:T(8,128)(2,1)S(1)}, u32[]{:S(2)}, u32[]{:S(2)}) collective-permute-start(f16[16,200,200]{2,1,0:T(8,128)(2,1)S(1)} %get-tuple-element.76), channel_id=1, source_target_pairs={{0,4},{4,0},{8,12},{12,8},{16,20},{20,16},{24,28},{28,24},{1,5},{5... | collective-permute-start | bytes 3840008 | tf_op jit(solution)/shard_map/ppermute | solution.py:252
  57.2 106.9 %collective-permute-start.5 = (f16[16,200,200]{2,1,0:T(8,128)(2,1)S(1)}, f16[16,200,200]{2,1,0:T(8,128)(2,1)S(1)}, u32[]{:S(2)}, u32[]{:S(2)}) collective-permute-start(f16[16,200,200]{2,1,0:T(8,128)(2,1)S(1)} %get-tuple-element.75), channel_id=1, source_target_pairs={{0,4},{4,0},{8,12},{12,8},{16,20},{20,16},{24,28},{28,24},{1,5},{5... | collective-permute-start | bytes 3840008 | tf_op jit(solution)/shard_map/ppermute | solution.py:252
  58.8 138.3 %collective-permute-start = (f16[16,200,200]{2,1,0:T(8,128)(2,1)}, f16[16,200,200]{2,1,0:T(8,128)(2,1)}, u32[]{:S(2)}, u32[]{:S(2)}) collective-permute-start(f16[16,200,200]{2,1,0:T(8,128)(2,1)} %get-tuple-element.74), channel_id=1, source_target_pairs={{0,4},{4,0},{8,12},{12,8},{16,20},{20,16},{24,28},{28,24},{1,5},{5... | collective-permute-start | bytes 3840008 | tf_op jit(solution)/shard_map/ppermute | solution.py:252
  171.6 37.1 %collective-permute-start.2 = (f16[16,200,200]{2,1,0:T(8,128)(2,1)}, f16[16,200,200]{2,1,0:T(8,128)(2,1)}, u32[]{:S(2)}, u32[]{:S(2)}) collective-permute-start(f16[16,200,200]{2,1,0:T(8,128)(2,1)} %get-tuple-element.78), channel_id=1, source_target_pairs={{0,8},{4,12},{8,16},{12,20},{16,24},{20,28},{24,0},{28,4},{1,9},{5... | collective-permute-start | bytes 3840008 | tf_op jit(solution)/shard_map/ppermute | solution.py:258
  172.2 138.5 %collective-permute-start.4 = (f16[16,200,200]{2,1,0:T(8,128)(2,1)}, f16[16,200,200]{2,1,0:T(8,128)(2,1)}, u32[]{:S(2)}, u32[]{:S(2)}) collective-permute-start(f16[16,200,200]{2,1,0:T(8,128)(2,1)} %get-tuple-element.80), channel_id=1, source_target_pairs={{0,16},{4,20},{8,24},{12,28},{16,0},{20,4},{24,8},{28,12},{1,17},{... | collective-permute-start | bytes 3840008 | tf_op jit(solution)/shard_map/ppermute | solution.py:258
  173.4 137.3 %collective-permute-start.6 = (f16[16,200,200]{2,1,0:T(8,128)(2,1)}, f16[16,200,200]{2,1,0:T(8,128)(2,1)}, u32[]{:S(2)}, u32[]{:S(2)}) collective-permute-start(f16[16,200,200]{2,1,0:T(8,128)(2,1)} %get-tuple-element.79), channel_id=1, source_target_pairs={{0,24},{4,28},{8,0},{12,4},{16,8},{20,12},{24,16},{28,20},{1,25},{... | collective-permute-start | bytes 3840008 | tf_op jit(solution)/shard_map/ppermute | solution.py:258
  310.7 8.5 %copy-start.12 = (f32[1,16,200,200]{3,2,1,0:T(8,128)S(1)}, f32[1,16,200,200]{3,2,1,0:T(8,128)}, u32[]{:S(2)}) copy-start(f32[1,16,200,200]{3,2,1,0:T(8,128)} %param.30) | copy-start | bytes 7680004
  319.2 3.6 copy-start.5
  319.2 3.6 copy-start.8
  347.6 10.3 %copy-start.17 = (f32[1600]{0:T(1024)S(1)}, f32[1600]{0:T(1024)}, u32[]{:S(2)}) copy-start(f32[1600]{0:T(1024)} %param.35) | copy-start | bytes 19204
  347.7 10.3 %copy-start.18 = (f32[1600]{0:T(1024)S(1)}, f32[1600]{0:T(1024)}, u32[]{:S(2)}) copy-start(f32[1600]{0:T(1024)} %param.36) | copy-start | bytes 19204
  347.7 10.3 %copy-start.19 = (f32[1600]{0:T(1024)S(1)}, f32[1600]{0:T(1024)}, u32[]{:S(2)}) copy-start(f32[1600]{0:T(1024)} %param.37) | copy-start | bytes 19204
  347.7 11.0 %copy-start.20 = (f32[1200]{0:T(1024)S(1)}, f32[1200]{0:T(1024)}, u32[]{:S(2)}) copy-start(f32[1200]{0:T(1024)} %param.32) | copy-start | bytes 14404
  347.7 11.0 %copy-start.21 = (f32[1200]{0:T(1024)S(1)}, f32[1200]{0:T(1024)}, u32[]{:S(2)}) copy-start(f32[1200]{0:T(1024)} %param.33) | copy-start | bytes 14404
  347.7 11.0 %copy-start.22 = (f32[1200]{0:T(1024)S(1)}, f32[1200]{0:T(1024)}, u32[]{:S(2)}) copy-start(f32[1200]{0:T(1024)} %param.34) | copy-start | bytes 14404
  347.7 13.0 %copy-start.6 = (f32[16,200,200]{2,1,0:T(8,128)S(1)}, f32[16,200,200]{2,1,0:T(8,128)}, u32[]{:S(2)}) copy-start(f32[16,200,200]{2,1,0:T(8,128)} %copy-done.5) | copy-start | bytes 7680004
  347.7 13.0 %copy-start.13 = (f32[1,16,200,200]{3,2,1,0:T(8,128)S(1)}, f32[1,16,200,200]{3,2,1,0:T(8,128)}, u32[]{:S(2)}) copy-start(f32[1,16,200,200]{3,2,1,0:T(8,128)} %param.29) | copy-start | bytes 7680004
  355.3 38.0 %collective-permute-start.7 = (bf16[16,200,200]{2,1,0:T(8,128)(2,1)}, bf16[16,200,200]{2,1,0:T(8,128)(2,1)}, u32[]{:S(2)}, u32[]{:S(2)}) collective-permute-start(bf16[16,200,200]{2,1,0:T(8,128)(2,1)} %get-tuple-element.69), channel_id=1, source_target_pairs={{0,8},{4,12},{8,16},{12,20},{16,24},{20,28},{24,0},{28,4},{1,9},{5... | collective-permute-start | bytes 3840008 | tf_op jit(solution)/shard_map/ppermute | solution.py:304
  356.7 141.0 %collective-permute-start.8 = (bf16[16,200,200]{2,1,0:T(8,128)(2,1)}, bf16[16,200,200]{2,1,0:T(8,128)(2,1)S(1)}, u32[]{:S(2)}, u32[]{:S(2)}) collective-permute-start(bf16[16,200,200]{2,1,0:T(8,128)(2,1)} %get-tuple-element.69), channel_id=1, source_target_pairs={{0,16},{4,20},{8,24},{12,28},{16,0},{20,4},{24,8},{28,12},{1,17},{... | collective-permute-start | bytes 3840008 | tf_op jit(solution)/shard_map/ppermute | solution.py:304
  357.3 147.0 %collective-permute-start.9 = (bf16[16,200,200]{2,1,0:T(8,128)(2,1)}, bf16[16,200,200]{2,1,0:T(8,128)(2,1)}, u32[]{:S(2)}, u32[]{:S(2)}) collective-permute-start(bf16[16,200,200]{2,1,0:T(8,128)(2,1)} %get-tuple-element.69), channel_id=1, source_target_pairs={{0,24},{4,28},{8,0},{12,4},{16,8},{20,12},{24,16},{28,20},{1,25},{... | collective-permute-start | bytes 3840008 | tf_op jit(solution)/shard_map/ppermute | solution.py:304
  359.3 139.5 %copy-start.14 = (f32[1,16,200,200]{3,2,1,0:T(8,128)S(1)}, f32[1,16,200,200]{3,2,1,0:T(8,128)}, u32[]{:S(2)}) copy-start(f32[1,16,200,200]{3,2,1,0:T(8,128)} %param.28) | copy-start | bytes 7680004
  359.3 151.5 %collective-permute-start.10 = (bf16[16,200,200]{2,1,0:T(8,128)(2,1)}, bf16[16,200,200]{2,1,0:T(8,128)(2,1)}, u32[]{:S(2)}, u32[]{:S(2)}) collective-permute-start(bf16[16,200,200]{2,1,0:T(8,128)(2,1)} %get-tuple-element.69), channel_id=1, source_target_pairs={{0,4},{4,0},{8,12},{12,8},{16,20},{20,16},{24,28},{28,24},{1,5},{5... | collective-permute-start | bytes 3840008 | tf_op jit(solution)/shard_map/ppermute | solution.py:305
  369.2 136.1 %copy-start.7 = (f32[16,200,200]{2,1,0:T(8,128)S(1)}, f32[16,200,200]{2,1,0:T(8,128)}, u32[]{:S(2)}) copy-start(f32[16,200,200]{2,1,0:T(8,128)} %get-tuple-element.96) | copy-start | bytes 7680004
  369.2 136.1 %copy-start.9 = (f32[1,16,200,200]{3,2,1,0:T(8,128)S(1)}, f32[1,16,200,200]{3,2,1,0:T(8,128)}, u32[]{:S(2)}) copy-start(f32[1,16,200,200]{3,2,1,0:T(8,128)} %param.26) | copy-start | bytes 7680004
  393.3 119.1 %collective-permute-start.11 = (bf16[16,200,200]{2,1,0:T(8,128)(2,1)}, bf16[16,200,200]{2,1,0:T(8,128)(2,1)S(1)}, u32[]{:S(2)}, u32[]{:S(2)}) collective-permute-start(bf16[16,200,200]{2,1,0:T(8,128)(2,1)} %collective-permute-done.7), channel_id=1, source_target_pairs={{0,4},{4,0},{8,12},{12,8},{16,20},{20,16},{24,28},{28,24},{1,5},{5... | collective-permute-start | bytes 3840008 | tf_op jit(solution)/shard_map/ppermute | solution.py:305
  497.7 38.7 %collective-permute-start.12 = (bf16[16,200,200]{2,1,0:T(8,128)(2,1)S(1)}, bf16[16,200,200]{2,1,0:T(8,128)(2,1)S(1)}, u32[]{:S(2)}, u32[]{:S(2)}) collective-permute-start(bf16[16,200,200]{2,1,0:T(8,128)(2,1)S(1)} %collective-permute-done.8), channel_id=1, source_target_pairs={{0,4},{4,0},{8,12},{12,8},{16,20},{20,16},{24,28},{28,24},{1,5},{5... | collective-permute-start | bytes 3840008 | tf_op jit(solution)/shard_map/ppermute | solution.py:305
  504.3 64.5 %collective-permute-start.13 = (bf16[16,200,200]{2,1,0:T(8,128)(2,1)}, bf16[16,200,200]{2,1,0:T(8,128)(2,1)S(1)}, u32[]{:S(2)}, u32[]{:S(2)}) collective-permute-start(bf16[16,200,200]{2,1,0:T(8,128)(2,1)} %collective-permute-done.9), channel_id=1, source_target_pairs={{0,4},{4,0},{8,12},{12,8},{16,20},{20,16},{24,28},{28,24},{1,5},{5... | collective-permute-start | bytes 3840008 | tf_op jit(solution)/shard_map/ppermute | solution.py:305
  571.3 4.7 copy-start.2
  576.0 1.9 copy-start.4
  577.9 4.7 copy-start.3
  582.6 8.7 %copy-start.1 = (f32[1,16,200,200]{3,2,1,0:T(8,128)S(1)}, f32[1,16,200,200]{3,2,1,0:T(8,128)}, u32[]{:S(2)}) copy-start(f32[1,16,200,200]{3,2,1,0:T(8,128)} %param.31) | copy-start | bytes 7680004

commit v2 on v1

--- a/solution.py
+++ b/solution.py
@@ -242,20 +242,28 @@
         return lax.dynamic_index_in_dim(array, where, 0, keepdims=False)
 
     across = [(d, d ^ 1) for d in range(groups)]
-    mine = None
     arrivals = []
-    for step_off in list(range(1, pairs)) + [0]:
-        target = lax.rem(pair + step_off, pairs)
-        theirs = target * 2 + 1 - side
-        ours = target * 2 + side
+    order = list(range(1, pairs))
+    if pairs == 4:
+        order = [1, 3, 2]
+    order = order + [0]
+    received = []
+    for step_off in order:
+        theirs = lax.rem(pair + step_off, pairs) * 2 + 1 - side
         sent = (chunk(tiles, theirs) * chunk(shrink, theirs)).astype(jnp.float16)
-        got = lax.ppermute(sent, "dp", across)
+        received.append(lax.ppermute(sent, "dp", across))
+    after = jnp.int32(0)
+    for step_off, got in zip(order, received):
+        ours = lax.rem(pair + step_off, pairs) * 2 + side + after
         both = chunk(tiles, ours) * chunk(shrink, ours) + got.astype(jnp.float32)
         if step_off == 0:
             mine = both
         else:
             hop = [(d, ((d // 2 + step_off) % pairs) * 2 + d % 2) for d in range(groups)]
-            arrivals.append(lax.ppermute(both.astype(jnp.float16), "dp", hop))
+            both = both.astype(jnp.float16)
+            arrivals.append(lax.ppermute(both, "dp", hop))
+            probe = arrivals[-1][0, 0, 0].astype(jnp.float32)
+            after = jnp.minimum((probe == probe).astype(jnp.int32), 0)
     for arrived in arrivals:
         mine = mine + arrived.astype(jnp.float32)
     grads = jnp.where(keep, mine * (chunk(grow, own_index) / tokens), 0.0)
@@ -299,15 +307,47 @@
     right_new = jnp.where(keep, new_r, old_r)
     new_weights = master_new.astype(jnp.bfloat16)
     spread = [new_weights]
-    for step_off in range(1, pairs):
-        hop = [(d, ((d // 2 + step_off) % pairs) * 2 + d % 2) for d in range(groups)]
-        spread.append(lax.ppermute(new_weights, "dp", hop))
-    other = [lax.ppermute(part_w, "dp", across) for part_w in spread]
+    turns = None
+    if pairs == 4:
+        up = [(d, d + 2) for d in range(groups - 2)]
+        down = [(d + 2, d) for d in range(groups - 2)]
+        from_low, from_high = [new_weights], [new_weights]
+        for k in range(1, pairs):
+            from_low.append(lax.ppermute(from_low[-1], "dp", up))
+            from_high.append(lax.ppermute(from_high[-1], "dp", down))
+        rows = []
+        for z in range(pairs):
+            found = [(k, 0) for k in range(1, z + 1)] + [(k, 1) for k in range(1, pairs - z)]
+            rows.append(sorted(found))
+        turns = [[0] * pairs for _ in range(pairs)]
+        other = [lax.ppermute(new_weights, "dp", across)]
+        for m in range(pairs - 1):
+            value = None
+            probe = other[-1][0, 0, 0].astype(jnp.float32)
+            here = pair + jnp.minimum((probe == probe).astype(jnp.int32), 0)
+            for z in range(pairs):
+                k, way = rows[z][m]
+                turns[z][z + k if way else z - k] = m + 1
+                part_w = (from_low, from_high)[way][k]
+                value = part_w if value is None else jnp.where(here == z, part_w, value)
+            spread.append(value)
+            other.append(lax.ppermute(value, "dp", across))
+    else:
+        for step_off in range(1, pairs):
+            hop = [(d, ((d // 2 + step_off) % pairs) * 2 + d % 2) for d in range(groups)]
+            spread.append(lax.ppermute(new_weights, "dp", hop))
+        other = [lax.ppermute(part_w, "dp", across) for part_w in spread]
     everyone = jnp.concatenate(spread + other)
     place_owner = owner // 2
     turn = lax.rem(pair - place_owner + pairs, pairs)
-    order = jnp.where(owner % 2 == side, turn, pairs + turn)
-    where_held = order * slot_count + (position - owner * slot_count)
+    if turns is not None:
+        turn = jnp.zeros_like(owner)
+        for z in range(pairs):
+            for origin in range(pairs):
+                hit = (pair == z) & (place_owner == origin)
+                turn = jnp.where(hit, turns[z][origin], turn)
+    held = jnp.where(owner % 2 == side, turn, pairs + turn)
+    where_held = held * slot_count + (position - owner * slot_count)
     qkv_weight = join_tiles(everyone, where_held, 0, rows_q, cols_q)
     proj_weight = join_tiles(everyone, where_held, first_kind, rows_p, rows_q)
     qb_new, qm_new, qv_new = adamw(

time: 592 us -> 487 us (0.82)
  the two profiles are of different devices: /device:TPU:24 before, /device:TPU:0 now
where the time goes in v2:
time: 487 us; the launch traced here: 486 us
  waiting for transfers between devices  280 us (57%)
  other arithmetic  64.1 us (13%)
  Pallas kernels  55.7 us (11%)
  local copies, waits for them, and re-layouts  30.2 us (6%)
  starting transfers between devices  24.8 us (5%)
  matrix products  23.4 us (5%)
  between operations  7.83 us (2%)
    ppermute x3, waiting for transfers between devices, on_device(): arrivals.append(lax.ppermute(both, 'dp', hop))  136 us
    ppermute x3, waiting for transfers between devices, on_device(): other.append(lax.ppermute(value, 'dp', across))  69 us
    ppermute x4, waiting for transfers between devices, on_device(): received.append(lax.ppermute(sent, 'dp', across))  35.1 us
    ppermute x1, waiting for transfers between devices, on_device(): other = [lax.ppermute(new_weights, 'dp', across)]  31 us
    pallas_call x1, Pallas kernels, place_tiles(): pl.pallas_call(lambda *refs: place_kernel(split, cols_q, rows_q, *refs),...  30.3 us
    pallas_call x2, Pallas kernels, sum_over(): pl.pallas_call(lambda *refs: sum_kernel(axes, sizes, *refs), out_shape=ja...  21.1 us
    unnamed x64, local copies, waits for them, and re-layouts  20.9 us
    unnamed x4, other arithmetic  18.6 us
  transfers between devices with their start and end apart: 17, of which 11 were waited for; matrix products, arithmetic and copies ran while one was open for 6% of the time, Pallas kernels for 0%

profile of v2, /device:TPU:0, one launch (start us, length us, event | category | flops | bytes accessed | tf_op | source)
XLA Modules:
  0.0 486.1 jit_solution(9158162060226346138)
XLA Ops:
  0.8 1.0 select_reduce_fusion.2
  1.8 1.8 convert_reduce_fusion
  3.6 1.7 convert_reduce_fusion.1
  6.2 30.3 %shard_map.282 = (f32[128,200,200]{2,1,0:T(8,128)}, f32[64,8,128]{2,1,0:T(8,128)S(1)}) custom-call(s32[64]{0:T(128)S(1)} %get-tuple-element.92.refs_0_, bf16[10,200,512]{2,1,0:T(8,128)(2,1)S(1)} %pad_maximum_fusion.1.refs_1_, bf16[14,200,512]{2,1,0:T(8,128)(2,1)S(1)} %pad_maximum_fusion.refs_2_), custom_call_target="tpu_custom_call" | custom-call | tf_op jit(solution)/shard_map/pallas_call | solution.py:52
  37.8 10.2 %shard_map.283 = f32[8,384]{1,0:T(8,128)} custom-call(f32[8,384]{1,0:T(8,128)} %reshape.161.refs_0_), custom_call_target="tpu_custom_call" | custom-call | tf_op jit(solution)/shard_map/pallas_call | solution.py:143
  49.0 8.0 %fusion.10 = (f16[16,200,200]{2,1,0:T(8,128)(2,1)}, f16[16,200,200]{2,1,0:T(8,128)(2,1)}, f16[16,200,200]{2,1,0:T(8,128)(2,1)}, f16[16,200,200]{2,1,0:T(8,128)(2,1)S(1)}) fusion(f32[8,16,200,200]{3,2,1,0:T(8,128)} %bitcast.164, s32[]{:T(128)S(6)} %select_n.264, f32[16]{0:T(128)S(1)} %get-tuple-element.84, f32[16]{0:T(128)S(1)} %get-tuple-element.85, ...), kind=kLoop, calls=%fused_computation.19 | loop fusion | flops 5120000 | bytes 15360272 | tf_op jit(solution)/shard_map/convert_element_type | solution.py:253
  57.0 1.6 collective-permute-start
  58.6 35.1 %collective-permute-done = f16[16,200,200]{2,1,0:T(8,128)(2,1)S(1)} collective-permute-done((f16[16,200,200]{2,1,0:T(8,128)(2,1)S(1)}, f16[16,200,200]{2,1,0:T(8,128)(2,1)S(1)}, u32[]{:S(2)}, u32[]{:S(2)}) %collective-permute-start) | collective-permute-done | bytes 1280032 | tf_op jit(solution)/shard_map/ppermute | solution.py:254
  93.6 3.8 fusion.25
  97.4 0.9 collective-permute-start.1
  98.4 1.3 collective-permute-start.2
  99.7 35.6 %collective-permute-done.1 = f16[16,200,200]{2,1,0:T(8,128)(2,1)} collective-permute-done((f16[16,200,200]{2,1,0:T(8,128)(2,1)}, f16[16,200,200]{2,1,0:T(8,128)(2,1)}, u32[]{:S(2)}, u32[]{:S(2)}) %collective-permute-start.1) | collective-permute-done | bytes 1280032 | tf_op jit(solution)/shard_map/ppermute | solution.py:264
  135.3 1.2 slice.59
  137.2 4.2 fusion.22
  141.3 1.1 collective-permute-start.3
  142.4 1.6 collective-permute-start.4
  144.0 32.5 %collective-permute-done.3 = f16[16,200,200]{2,1,0:T(8,128)(2,1)} collective-permute-done((f16[16,200,200]{2,1,0:T(8,128)(2,1)}, f16[16,200,200]{2,1,0:T(8,128)(2,1)}, u32[]{:S(2)}, u32[]{:S(2)}) %collective-permute-start.3) | collective-permute-done | bytes 1280032 | tf_op jit(solution)/shard_map/ppermute | solution.py:264
  176.5 1.2 slice.60
  178.4 4.2 fusion.19
  182.8 1.0 collective-permute-start.6
  184.9 67.8 %collective-permute-done.5 = f16[16,200,200]{2,1,0:T(8,128)(2,1)} collective-permute-done((f16[16,200,200]{2,1,0:T(8,128)(2,1)}, f16[16,200,200]{2,1,0:T(8,128)(2,1)}, u32[]{:S(2)}, u32[]{:S(2)}) %collective-permute-start.5) | collective-permute-done | bytes 1280032 | tf_op jit(solution)/shard_map/ppermute | solution.py:264
  252.6 1.2 slice.61
  254.5 8.5 %fusion.5 = (f32[1,16,200,200]{3,2,1,0:T(8,128)}, f32[16,200,200]{2,1,0:T(8,128)S(1)}) fusion(f32[1,16,200,200]{3,2,1,0:T(8,128)} %param.27, pred[16]{0:T(512)(128)(4,1)S(1)} %dynamic_slice.59, f32[16]{0:T(128)S(1)} %fusion.44, f16[16,200,200]{2,1,0:T(8,128)(2,1)} %collective-permute-done.5, f16[16,200,200]{2,1,0:T(8,128)(2,1)} %collective-permute-done.3, ...), kind=kLoop, calls=%fused_computation.13 | loop fusion | flops 10240000 | bytes 15360148 | tf_op jit(solution)/shard_map/broadcast_in_dim | solution.py:362
  263.0 3.6 fusion.8
  266.6 2.0 multiply_reduce_fusion
  268.6 5.4 %multiply_reduce_fusion.1 = (f32[16]{0:T(128)S(1)}, f32[16,200,200]{2,1,0:T(8,128)}) fusion(f32[16,200,200]{1,2,0:T(8,128)S(1)} %fusion.8, f32[1,16,200,200]{3,2,1,0:T(8,128)S(1)} %copy-done), kind=kOutput, calls=%fused_computation.50 | convolution fusion | flops 1537280000 | bytes 7680064 | tf_op jit(solution)/shard_map/sij,sjk->sik/dot_general | solution.py:278
  275.4 2.5 select_select_fusion.3.refs_0_
  277.9 10.9 %shard_map.284 = f32[8,128]{1,0:T(8,128)} custom-call(f32[8,128]{1,0:T(8,128)} %select_select_fusion.3.refs_0_), custom_call_target="tpu_custom_call" | custom-call | tf_op jit(solution)/shard_map/pallas_call | solution.py:143
  290.3 1.3 broadcast_select_fusion
  291.6 7.2 %constant_dynamic-update-slice_fusion.7 = (bf16[128,200,200]{2,1,0:T(8,128)(2,1)}, bf16[16,200,200]{2,1,0:T(8,128)(2,1)S(1)}, f32[16,200,200]{2,1,0:T(8,128)}) fusion(f32[16,200,200]{2,1,0:T(8,128)} %get-tuple-element.96, f32[16]{0:T(128)S(1)} %broadcast_select_fusion, f32[1,16,200,200]{3,2,1,0:T(8,128)} %param.26, f32[1,16,200,200]{3,2,1,0:T(8,128)} %param.25, ...), kind=kLoop, calls=%fused_computation.74 | loop fusion | flops 6399999 | bytes 13875280
  298.8 0.9 collective-permute-start.7
  299.8 3.7 collective-permute-start.8
  303.5 1.3 collective-permute-start.9
  304.8 31.0 %collective-permute-done.7 = bf16[16,200,200]{2,1,0:T(8,128)(2,1)S(1)} collective-permute-done((bf16[16,200,200]{2,1,0:T(8,128)(2,1)S(1)}, bf16[16,200,200]{2,1,0:T(8,128)(2,1)S(1)}, u32[]{:S(2)}, u32[]{:S(2)}) %collective-permute-start.7) | collective-permute-done | bytes 1280032 | tf_op jit(solution)/shard_map/ppermute | solution.py:323
  335.8 1.2 copy-done.15
  338.8 3.0 collective-permute-done.9
  341.8 3.8 constant_dynamic-update-slice_fusion.6
  345.5 1.1 collective-permute-start.10
  346.6 2.9 collective-permute-start.11
  349.5 1.3 collective-permute-start.12
  350.8 30.2 %collective-permute-done.10 = bf16[16,200,200]{2,1,0:T(8,128)(2,1)S(1)} collective-permute-done((bf16[16,200,200]{2,1,0:T(8,128)(2,1)S(1)}, bf16[16,200,200]{2,1,0:T(8,128)(2,1)S(1)}, u32[]{:S(2)}, u32[]{:S(2)}) %collective-permute-start.10) | collective-permute-done | bytes 1280032 | tf_op jit(solution)/shard_map/ppermute | solution.py:334
  382.9 3.8 collective-permute-done.12
  386.8 3.9 constant_dynamic-update-slice_fusion.5
  390.7 0.9 collective-permute-start.13
  391.6 2.5 collective-permute-start.14
  394.1 1.3 collective-permute-start.15
  396.8 8.7 %fusion.2 = f32[1,16,200,200]{3,2,1,0:T(8,128)} fusion(f32[1,16,200,200]{3,2,1,0:T(8,128)S(1)} %copy-done.13, f32[16,200,200]{2,1,0:T(8,128)S(1)} %copy-done.5, pred[16]{0:T(512)(128)(4,1)S(1)} %dynamic_slice.59), kind=kOutput, calls=%fused_computation.6 | convolution fusion | flops 1538560000 | bytes 7680016 | tf_op jit(solution)/shard_map/ski,skj->sij/dot_general | solution.py:300
  405.5 19.5 %collective-permute-done.13 = bf16[16,200,200]{2,1,0:T(8,128)(2,1)S(1)} collective-permute-done((bf16[16,200,200]{2,1,0:T(8,128)(2,1)S(1)}, bf16[16,200,200]{2,1,0:T(8,128)(2,1)S(1)}, u32[]{:S(2)}, u32[]{:S(2)}) %collective-permute-start.13) | collective-permute-done | bytes 1280032 | tf_op jit(solution)/shard_map/ppermute | solution.py:334
  425.0 1.2 copy-done.19
  428.0 2.3 collective-permute-done.15
  430.3 3.6 constant_dynamic-update-slice_fusion.4
  433.9 1.1 collective-permute-start.16
  435.0 2.3 fusion.27
  437.4 5.7 %fusion.4 = f32[1,16,200,200]{3,2,1,0:T(8,128)} fusion(f32[1,16,200,200]{3,2,1,0:T(8,128)S(1)} %copy-done.14, f32[16,200,200]{2,1,0:T(8,128)S(1)} %copy-done.5, pred[16]{0:T(512)(128)(4,1)S(1)} %dynamic_slice.59), kind=kOutput, calls=%fused_computation.10 | convolution fusion | flops 1538560000 | bytes 7680016 | tf_op jit(solution)/shard_map/sik,sjk->sij/dot_general | solution.py:297
  443.1 1.3 constant_dynamic-update-slice_fusion.3
  445.1 1.3 constant_dynamic-update-slice_fusion.2
  446.4 1.3 constant_dynamic-update-slice_fusion.1
  447.7 19.3 %collective-permute-done.16 = bf16[16,200,200]{2,1,0:T(8,128)(2,1)S(1)} collective-permute-done((bf16[16,200,200]{2,1,0:T(8,128)(2,1)S(1)}, bf16[16,200,200]{2,1,0:T(8,128)(2,1)S(1)}, u32[]{:S(2)}, u32[]{:S(2)}) %collective-permute-start.16) | collective-permute-done | bytes 1280032 | tf_op jit(solution)/shard_map/ppermute | solution.py:334
  467.0 1.4 constant_dynamic-update-slice_fusion.refs_1_.refs_2_.refs_3_.refs_4_.refs_5_.refs_6_.refs_7_.refs_8_
  468.4 4.7 copy-done.2
  473.1 2.3 shard_map.285
  475.4 1.9 copy-done.3
  477.4 2.0 shard_map.286
  479.3 6.7 %copy.39 = bf16[1600,1200]{0,1:T(8,128)(2,1)} copy(bf16[1600,1200]{1,0:T(8,128)(2,1)} %copy-done.3) | data formatting | bytes 7680000
  (94 shorter events, 10.2 us)
Async XLA Ops:
  0.6 268.0 %copy-start = (f32[1,16,200,200]{3,2,1,0:T(8,128)S(1)}, f32[1,16,200,200]{3,2,1,0:T(8,128)}, u32[]{:S(2)}) copy-start(f32[1,16,200,200]{3,2,1,0:T(8,128)} %param.31) | copy-start | bytes 7680004
  0.8 4.5 copy-start.9
  0.8 4.5 copy-start.11
  3.5 2.0 copy-start.21
  3.5 2.0 copy-start.22
  5.5 0.7 copy-start.29
  57.0 36.7 %collective-permute-start = (f16[16,200,200]{2,1,0:T(8,128)(2,1)S(1)}, f16[16,200,200]{2,1,0:T(8,128)(2,1)S(1)}, u32[]{:S(2)}, u32[]{:S(2)}) collective-permute-start(f16[16,200,200]{2,1,0:T(8,128)(2,1)S(1)} %get-tuple-element.83), channel_id=1, source_target_pairs={{0,4},{4,0},{8,12},{12,8},{16,20},{20,16},{24,28},{28,24},{1,5},{5... | collective-permute-start | bytes 3840008 | tf_op jit(solution)/shard_map/ppermute | solution.py:254
  97.4 37.9 %collective-permute-start.1 = (f16[16,200,200]{2,1,0:T(8,128)(2,1)}, f16[16,200,200]{2,1,0:T(8,128)(2,1)}, u32[]{:S(2)}, u32[]{:S(2)}) collective-permute-start(f16[16,200,200]{2,1,0:T(8,128)(2,1)} %fusion.25), channel_id=1, source_target_pairs={{0,8},{4,12},{8,16},{12,20},{16,24},{20,28},{24,0},{28,4},{1,9},{5... | collective-permute-start | bytes 3840008 | tf_op jit(solution)/shard_map/ppermute | solution.py:264
  98.4 38.8 %collective-permute-start.2 = (f16[16,200,200]{2,1,0:T(8,128)(2,1)}, f16[16,200,200]{2,1,0:T(8,128)(2,1)}, u32[]{:S(2)}, u32[]{:S(2)}) collective-permute-start(f16[16,200,200]{2,1,0:T(8,128)(2,1)} %get-tuple-element.82), channel_id=1, source_target_pairs={{0,4},{4,0},{8,12},{12,8},{16,20},{20,16},{24,28},{28,24},{1,5},{5... | collective-permute-start | bytes 3840008 | tf_op jit(solution)/shard_map/ppermute | solution.py:254
  141.3 35.2 %collective-permute-start.3 = (f16[16,200,200]{2,1,0:T(8,128)(2,1)}, f16[16,200,200]{2,1,0:T(8,128)(2,1)}, u32[]{:S(2)}, u32[]{:S(2)}) collective-permute-start(f16[16,200,200]{2,1,0:T(8,128)(2,1)} %fusion.22), channel_id=1, source_target_pairs={{0,24},{4,28},{8,0},{12,4},{16,8},{20,12},{24,16},{28,20},{1,25},{... | collective-permute-start | bytes 3840008 | tf_op jit(solution)/shard_map/ppermute | solution.py:264
  142.4 36.0 %collective-permute-start.4 = (f16[16,200,200]{2,1,0:T(8,128)(2,1)}, f16[16,200,200]{2,1,0:T(8,128)(2,1)}, u32[]{:S(2)}, u32[]{:S(2)}) collective-permute-start(f16[16,200,200]{2,1,0:T(8,128)(2,1)} %get-tuple-element.81), channel_id=1, source_target_pairs={{0,4},{4,0},{8,12},{12,8},{16,20},{20,16},{24,28},{28,24},{1,5},{5... | collective-permute-start | bytes 3840008 | tf_op jit(solution)/shard_map/ppermute | solution.py:254
  182.6 70.1 %collective-permute-start.5 = (f16[16,200,200]{2,1,0:T(8,128)(2,1)}, f16[16,200,200]{2,1,0:T(8,128)(2,1)}, u32[]{:S(2)}, u32[]{:S(2)}) collective-permute-start(f16[16,200,200]{2,1,0:T(8,128)(2,1)} %fusion.19), channel_id=1, source_target_pairs={{0,16},{4,20},{8,24},{12,28},{16,0},{20,4},{24,8},{28,12},{1,17},{... | collective-permute-start | bytes 3840008 | tf_op jit(solution)/shard_map/ppermute | solution.py:264
  182.8 71.6 %collective-permute-start.6 = (f16[16,200,200]{2,1,0:T(8,128)(2,1)}, f16[16,200,200]{2,1,0:T(8,128)(2,1)}, u32[]{:S(2)}, u32[]{:S(2)}) collective-permute-start(f16[16,200,200]{2,1,0:T(8,128)(2,1)} %get-tuple-element.80), channel_id=1, source_target_pairs={{0,4},{4,0},{8,12},{12,8},{16,20},{20,16},{24,28},{28,24},{1,5},{5... | collective-permute-start | bytes 3840008 | tf_op jit(solution)/shard_map/ppermute | solution.py:254
  254.5 8.5 %copy-start.12 = (f32[1,16,200,200]{3,2,1,0:T(8,128)S(1)}, f32[1,16,200,200]{3,2,1,0:T(8,128)}, u32[]{:S(2)}) copy-start(f32[1,16,200,200]{3,2,1,0:T(8,128)} %param.30) | copy-start | bytes 7680004
  263.0 3.6 copy-start.4
  263.0 3.6 copy-start.7
  298.8 36.9 %collective-permute-start.7 = (bf16[16,200,200]{2,1,0:T(8,128)(2,1)S(1)}, bf16[16,200,200]{2,1,0:T(8,128)(2,1)S(1)}, u32[]{:S(2)}, u32[]{:S(2)}) collective-permute-start(bf16[16,200,200]{2,1,0:T(8,128)(2,1)S(1)} %get-tuple-element.75), channel_id=1, source_target_pairs={{0,4},{4,0},{8,12},{12,8},{16,20},{20,16},{24,28},{28,24},{1,5},{5... | collective-permute-start | bytes 3840008 | tf_op jit(solution)/shard_map/ppermute | solution.py:323
  299.8 39.0 %collective-permute-start.8 = (bf16[16,200,200]{2,1,0:T(8,128)(2,1)S(1)}, bf16[16,200,200]{2,1,0:T(8,128)(2,1)}, u32[]{:S(2)}, u32[]{:S(2)}) collective-permute-start(bf16[16,200,200]{2,1,0:T(8,128)(2,1)S(1)} %get-tuple-element.75), channel_id=1, source_target_pairs={{0,8},{4,12},{8,16},{12,20},{16,24},{20,28},{1,9},{5,13},{9,17},{1... | collective-permute-start | bytes 3840008 | tf_op jit(solution)/shard_map/ppermute | solution.py:316
  303.5 38.3 %collective-permute-start.9 = (bf16[16,200,200]{2,1,0:T(8,128)(2,1)S(1)}, bf16[16,200,200]{2,1,0:T(8,128)(2,1)S(1)}, u32[]{:S(2)}, u32[]{:S(2)}) collective-permute-start(bf16[16,200,200]{2,1,0:T(8,128)(2,1)S(1)} %get-tuple-element.75), channel_id=1, source_target_pairs={{8,0},{12,4},{16,8},{20,12},{24,16},{28,20},{9,1},{13,5},{17,9},{2... | collective-permute-start | bytes 3840008 | tf_op jit(solution)/shard_map/ppermute | solution.py:317
  335.8 1.2 copy-start.15
  341.8 7.7 %copy-start.10 = (bf16[16,200,200]{2,1,0:T(8,128)(2,1)}, bf16[16,200,200]{2,1,0:T(8,128)(2,1)S(1)}, u32[]{:S(2)}) copy-start(bf16[16,200,200]{2,1,0:T(8,128)(2,1)S(1)} %collective-permute-done.9) | copy-start | bytes 3840004
  345.5 35.5 %collective-permute-start.10 = (bf16[16,200,200]{2,1,0:T(8,128)(2,1)S(1)}, bf16[16,200,200]{2,1,0:T(8,128)(2,1)S(1)}, u32[]{:S(2)}, u32[]{:S(2)}) collective-permute-start(bf16[16,200,200]{2,1,0:T(8,128)(2,1)S(1)} %get-tuple-element.73), channel_id=1, source_target_pairs={{0,4},{4,0},{8,12},{12,8},{16,20},{20,16},{24,28},{28,24},{1,5},{5... | collective-permute-start | bytes 3840008 | tf_op jit(solution)/shard_map/ppermute | solution.py:334
  346.6 36.2 %collective-permute-start.11 = (bf16[16,200,200]{2,1,0:T(8,128)(2,1)}, bf16[16,200,200]{2,1,0:T(8,128)(2,1)}, u32[]{:S(2)}, u32[]{:S(2)}) collective-permute-start(bf16[16,200,200]{2,1,0:T(8,128)(2,1)} %collective-permute-done.8), channel_id=1, source_target_pairs={{0,8},{4,12},{8,16},{12,20},{16,24},{20,28},{1,9},{5,13},{9,17},{1... | collective-permute-start | bytes 3840008 | tf_op jit(solution)/shard_map/ppermute | solution.py:316
  349.5 37.2 %collective-permute-start.12 = (bf16[16,200,200]{2,1,0:T(8,128)(2,1)S(1)}, bf16[16,200,200]{2,1,0:T(8,128)(2,1)}, u32[]{:S(2)}, u32[]{:S(2)}) collective-permute-start(bf16[16,200,200]{2,1,0:T(8,128)(2,1)S(1)} %collective-permute-done.9), channel_id=1, source_target_pairs={{8,0},{12,4},{16,8},{20,12},{24,16},{28,20},{9,1},{13,5},{17,9},{2... | collective-permute-start | bytes 3840008 | tf_op jit(solution)/shard_map/ppermute | solution.py:317
  381.0 5.7 %copy-start.17 = (bf16[16,200,200]{2,1,0:T(8,128)(2,1)}, bf16[16,200,200]{2,1,0:T(8,128)(2,1)S(1)}, u32[]{:S(2)}) copy-start(bf16[16,200,200]{2,1,0:T(8,128)(2,1)S(1)} %collective-permute-done.10) | copy-start | bytes 3840004
  386.7 8.7 %copy-start.23 = (f32[1600]{0:T(1024)S(1)}, f32[1600]{0:T(1024)}, u32[]{:S(2)}) copy-start(f32[1600]{0:T(1024)} %param.35) | copy-start | bytes 19204
  386.7 8.7 %copy-start.24 = (f32[1600]{0:T(1024)S(1)}, f32[1600]{0:T(1024)}, u32[]{:S(2)}) copy-start(f32[1600]{0:T(1024)} %param.36) | copy-start | bytes 19204
  386.7 8.7 %copy-start.25 = (f32[1600]{0:T(1024)S(1)}, f32[1600]{0:T(1024)}, u32[]{:S(2)}) copy-start(f32[1600]{0:T(1024)} %param.37) | copy-start | bytes 19204
  386.7 9.5 %copy-start.26 = (f32[1200]{0:T(1024)S(1)}, f32[1200]{0:T(1024)}, u32[]{:S(2)}) copy-start(f32[1200]{0:T(1024)} %param.32) | copy-start | bytes 14404
  386.7 9.4 %copy-start.27 = (f32[1200]{0:T(1024)S(1)}, f32[1200]{0:T(1024)}, u32[]{:S(2)}) copy-start(f32[1200]{0:T(1024)} %param.33) | copy-start | bytes 14404
  386.7 9.4 %copy-start.28 = (f32[1200]{0:T(1024)S(1)}, f32[1200]{0:T(1024)}, u32[]{:S(2)}) copy-start(f32[1200]{0:T(1024)} %param.34) | copy-start | bytes 14404
  386.7 10.1 %copy-start.5 = (f32[16,200,200]{2,1,0:T(8,128)S(1)}, f32[16,200,200]{2,1,0:T(8,128)}, u32[]{:S(2)}) copy-start(f32[16,200,200]{2,1,0:T(8,128)} %copy-done.4) | copy-start | bytes 7680004
  386.7 10.0 %copy-start.13 = (f32[1,16,200,200]{3,2,1,0:T(8,128)S(1)}, f32[1,16,200,200]{3,2,1,0:T(8,128)}, u32[]{:S(2)}) copy-start(f32[1,16,200,200]{3,2,1,0:T(8,128)} %param.29) | copy-start | bytes 7680004
  390.7 34.3 %collective-permute-start.13 = (bf16[16,200,200]{2,1,0:T(8,128)(2,1)S(1)}, bf16[16,200,200]{2,1,0:T(8,128)(2,1)S(1)}, u32[]{:S(2)}, u32[]{:S(2)}) collective-permute-start(bf16[16,200,200]{2,1,0:T(8,128)(2,1)S(1)} %get-tuple-element.71), channel_id=1, source_target_pairs={{0,4},{4,0},{8,12},{12,8},{16,20},{20,16},{24,28},{28,24},{1,5},{5... | collective-permute-start | bytes 3840008 | tf_op jit(solution)/shard_map/ppermute | solution.py:334
  391.6 36.4 %collective-permute-start.14 = (bf16[16,200,200]{2,1,0:T(8,128)(2,1)}, bf16[16,200,200]{2,1,0:T(8,128)(2,1)}, u32[]{:S(2)}, u32[]{:S(2)}) collective-permute-start(bf16[16,200,200]{2,1,0:T(8,128)(2,1)} %collective-permute-done.11), channel_id=1, source_target_pairs={{0,8},{4,12},{8,16},{12,20},{16,24},{20,28},{1,9},{5,13},{9,17},{1... | collective-permute-start | bytes 3840008 | tf_op jit(solution)/shard_map/ppermute | solution.py:316
  394.1 36.2 %collective-permute-start.15 = (bf16[16,200,200]{2,1,0:T(8,128)(2,1)}, bf16[16,200,200]{2,1,0:T(8,128)(2,1)}, u32[]{:S(2)}, u32[]{:S(2)}) collective-permute-start(bf16[16,200,200]{2,1,0:T(8,128)(2,1)} %collective-permute-done.12), channel_id=1, source_target_pairs={{8,0},{12,4},{16,8},{20,12},{24,16},{28,20},{9,1},{13,5},{17,9},{2... | collective-permute-start | bytes 3840008 | tf_op jit(solution)/shard_map/ppermute | solution.py:317
  425.0 1.2 copy-start.19
  430.3 4.7 copy-start.6
  430.3 4.7 copy-start.8
  433.9 3.4 copy-start.14
  433.9 33.1 %collective-permute-start.16 = (bf16[16,200,200]{2,1,0:T(8,128)(2,1)S(1)}, bf16[16,200,200]{2,1,0:T(8,128)(2,1)S(1)}, u32[]{:S(2)}, u32[]{:S(2)}) collective-permute-start(bf16[16,200,200]{2,1,0:T(8,128)(2,1)S(1)} %get-tuple-element.69), channel_id=1, source_target_pairs={{0,4},{4,0},{8,12},{12,8},{16,20},{20,16},{24,28},{28,24},{1,5},{5... | collective-permute-start | bytes 3840008 | tf_op jit(solution)/shard_map/ppermute | solution.py:334
  437.4 5.7 %copy-start.16 = (bf16[16,200,200]{2,1,0:T(8,128)(2,1)S(1)}, bf16[16,200,200]{2,1,0:T(8,128)(2,1)}, u32[]{:S(2)}) copy-start(bf16[16,200,200]{2,1,0:T(8,128)(2,1)} %copy-done.15) | copy-start | bytes 3840004
  443.1 2.0 copy-start.18
  443.1 3.3 copy-start.20
  468.4 4.7 copy-start.2
  475.4 1.9 copy-start.3
  477.4 8.7 %copy-start.1 = (f32[1,16,200,200]{3,2,1,0:T(8,128)S(1)}, f32[1,16,200,200]{3,2,1,0:T(8,128)}, u32[]{:S(2)}) copy-start(f32[1,16,200,200]{3,2,1,0:T(8,128)} %param.31) | copy-start | bytes 7680004

commit v3 on v2

--- a/solution.py
+++ b/solution.py
@@ -33,42 +33,53 @@
     return (new_p, new_m, new_v)
 
 
-def place_kernel(split, cols_q, rows_q, pos_ref, left_ref, right_ref, tile_ref, peak_ref):
-    b = pl.program_id(0)
-    first = b < split
-    later = jnp.maximum(b - split, 0)
-    i = jnp.where(first, b // cols_q, rows_q + later // rows_q)
-    j = jnp.where(first, b % cols_q, cols_q + later % rows_q)
-    tile = lax.dot_general(
-        left_ref[i], right_ref[j], (((1,), (1,)), ((), ())), preferred_element_type=jnp.float32
-    )
-    tile_ref[0] = tile
-    peak_ref[0] = jnp.full((8, 128), jnp.max(jnp.abs(tile)), jnp.float32)
-
-
-def place_tiles(left, right, position, split, cols_q, rows_q, spots):
-    total = position.shape[0]
+def place_kernel(
+    split, cols_q, rows_q, slots, holder_ref, used_ref, left_ref, right_ref, tile_ref, peak_ref
+):
+    o = pl.program_id(0)
+    peak_ref[...] = jnp.zeros_like(peak_ref)
+    side = left_ref.shape[1]
+    for s in range(slots):
+        b = holder_ref[o * slots + s]
+
+        @pl.when(used_ref[o * slots + s] > 0)
+        def _():
+            first = b < split
+            later = jnp.maximum(b - split, 0)
+            i = jnp.where(first, b // cols_q, rows_q + later // rows_q)
+            j = jnp.where(first, b % cols_q, cols_q + later % rows_q)
+            tile = lax.dot_general(
+                left_ref[i],
+                right_ref[j],
+                (((1,), (1,)), ((), ())),
+                preferred_element_type=jnp.float32,
+            )
+            tile_ref[0, :, s * side : (s + 1) * side] = tile
+            peak_ref[0, s : s + 1, :] = jnp.full((1, 128), jnp.max(jnp.abs(tile)), jnp.float32)
+
+
+def place_tiles(left, right, holder, used, split, cols_q, rows_q, groups, slots):
     side, depth = left.shape[1:]
     return pl.pallas_call(
-        lambda *refs: place_kernel(split, cols_q, rows_q, *refs),
+        lambda *refs: place_kernel(split, cols_q, rows_q, slots, *refs),
         out_shape=(
-            jax.ShapeDtypeStruct((spots, side, side), jnp.float32),
-            jax.ShapeDtypeStruct((total, 8, 128), jnp.float32),
+            jax.ShapeDtypeStruct((groups, side, slots * side), jnp.float32),
+            jax.ShapeDtypeStruct((groups, slots, 128), jnp.float32),
         ),
         grid_spec=pltpu.PrefetchScalarGridSpec(
-            num_scalar_prefetch=1,
-            grid=(total,),
+            num_scalar_prefetch=2,
+            grid=(groups,),
             in_specs=[
-                pl.BlockSpec(left.shape, lambda b, pos: (0, 0, 0)),
-                pl.BlockSpec(right.shape, lambda b, pos: (0, 0, 0)),
+                pl.BlockSpec(left.shape, lambda o, h, u: (0, 0, 0)),
+                pl.BlockSpec(right.shape, lambda o, h, u: (0, 0, 0)),
             ],
             out_specs=[
-                pl.BlockSpec((1, side, side), lambda b, pos: (pos[b], 0, 0)),
-                pl.BlockSpec((1, 8, 128), lambda b, pos: (b, 0, 0)),
+                pl.BlockSpec((1, side, slots * side), lambda o, h, u: (o, 0, 0)),
+                pl.BlockSpec((1, slots, 128), lambda o, h, u: (o, 0, 0)),
             ],
         ),
         compiler_params=pltpu.CompilerParams(vmem_limit_bytes=32 * 1024 * 1024),
-    )(position, left, right)
+    )(holder, used, left, right)
 
 
 def join_kernel(count, pos_ref, *refs):
@@ -210,7 +221,15 @@
         ]
     )
     local_tiles, peaks = place_tiles(
-        left, right, position, first_kind, cols_q, rows_q, spots
+        left,
+        right,
+        holder,
+        filled.astype(jnp.int32),
+        first_kind,
+        cols_q,
+        rows_q,
+        groups,
+        slot_count,
     )
 
     width_q, width_p = grad_qkv.shape[1], grad_out.shape[1]
@@ -218,7 +237,7 @@
         [
             jnp.sum(grad_qkv, axis=0, dtype=jnp.float32),
             jnp.sum(grad_out, axis=0, dtype=jnp.float32),
-            peaks[:, 0, 0],
+            peaks[:, :, 0].reshape(spots),
         ]
     )
     used = small.shape[0]
@@ -228,15 +247,15 @@
     qkv_total = small[:width_q]
     proj_total = small[width_q : width_q + width_p]
     bound = small[width_q + width_p : used]
-    spot_bound = jnp.sum(jnp.where(matches, bound[None, :], 0.0), axis=1)
-    spot_bound = jnp.where(spot_bound > 0.0, spot_bound, 1.0).reshape(groups, slot_count, 1, 1)
+    spot_bound = jnp.where(bound > 0.0, bound, 1.0).reshape(groups, 1, slot_count)
+    spot_bound = jnp.repeat(spot_bound, block_size, axis=2)
     shrink = 16384.0 / spot_bound
     grow = spot_bound / 16384.0
 
     pair = own_index // 2
     side = own_index % 2
     pairs = groups // 2
-    tiles = local_tiles.reshape(groups, slot_count, block_size, block_size)
+    tiles = local_tiles
 
     def chunk(array, where):
         return lax.dynamic_index_in_dim(array, where, 0, keepdims=False)
@@ -254,19 +273,21 @@
         received.append(lax.ppermute(sent, "dp", across))
     after = jnp.int32(0)
     for step_off, got in zip(order, received):
-        ours = lax.rem(pair + step_off, pairs) * 2 + side + after
-        both = chunk(tiles, ours) * chunk(shrink, ours) + got.astype(jnp.float32)
+        ours = lax.rem(pair + step_off, pairs) * 2 + side
+        both = chunk(tiles, ours + after) * chunk(shrink, ours) + got.astype(jnp.float32)
         if step_off == 0:
             mine = both
         else:
             hop = [(d, ((d // 2 + step_off) % pairs) * 2 + d % 2) for d in range(groups)]
             both = both.astype(jnp.float16)
             arrivals.append(lax.ppermute(both, "dp", hop))
-            probe = arrivals[-1][0, 0, 0].astype(jnp.float32)
+            probe = arrivals[-1][0, 0].astype(jnp.float32)
             after = jnp.minimum((probe == probe).astype(jnp.int32), 0)
     for arrived in arrivals:
         mine = mine + arrived.astype(jnp.float32)
-    grads = jnp.where(keep, mine * (chunk(grow, own_index) / tokens), 0.0)
+    mine = mine * (chunk(grow, own_index) / tokens)
+    mine = mine.reshape(block_size, slot_count, block_size).transpose(1, 0, 2)
+    grads = jnp.where(keep, mine, 0.0)
     old_w = master[0]
     old_m = moment[0]
     old_v = second[0]

time: 487 us -> 458 us (0.940); the launches traced: 486 us -> 451 us
  waiting for transfers between devices: 280 us -> 232 us
  matrix products: 23.4 us -> 36 us
  local copies, waits for them, and re-layouts: 30.2 us -> 37.3 us
    ppermute x3, waiting for transfers between devices: 136 us -> 105 us  [on_device(): arrivals.append(lax.ppermute(both, 'dp', hop))]
    ppermute x3, waiting for transfers between devices: 69 us -> 59 us  [on_device(): other.append(lax.ppermute(value, 'dp', across))]
    ppermute x4, waiting for transfers between devices: 35.1 us -> 27.4 us  [on_device(): received.append(lax.ppermute(sent, 'dp', across))]
    reshape x0 -> x1, local copies, waits for them, and re-layouts: none -> 6.91 us  [on_device(): mine = mine.reshape(block_size, slot_count, block_size).transpose(1, 0, 2)]
    mul x0 -> x1, other arithmetic: none -> 5.59 us  [on_device(): mine = mine * (chunk(grow, own_index) / tokens)]
    dot_general x1, matrix products: 3.58 us -> 8.56 us  [on_device(): half = jnp.einsum('sij,sjk->sik', root_left[0], grads, precision=exact)]
    unnamed x64 -> x62, local copies, waits for them, and re-layouts: 20.9 us -> 21.7 us
  transfers between devices with their start and end apart: 17 -> 17, of which waited for: 11 -> 11; matrix products, arithmetic and copies ran while one was open for 6% -> 8% of each run, Pallas kernels for 0% -> 0%
where the time goes in v3:
time: 458 us; the launch traced here: 451 us
  waiting for transfers between devices  232 us (51%)
  other arithmetic  60 us (13%)
  Pallas kernels  51.9 us (11%)
  local copies, waits for them, and re-layouts  37.3 us (8%)
  matrix products  36 us (8%)
  starting transfers between devices  25.2 us (6%)
  between operations  8.4 us (2%)
    ppermute x3, waiting for transfers between devices, on_device(): arrivals.append(lax.ppermute(both, 'dp', hop))  105 us
    ppermute x3, waiting for transfers between devices, on_device(): other.append(lax.ppermute(value, 'dp', across))  59 us
    ppermute x1, waiting for transfers between devices, on_device(): other = [lax.ppermute(new_weights, 'dp', across)]  31.3 us
    ppermute x4, waiting for transfers between devices, on_device(): received.append(lax.ppermute(sent, 'dp', across))  27.4 us
    pallas_call x1, Pallas kernels, place_tiles(): pl.pallas_call(lambda *refs: place_kernel(split, cols_q, rows_q, slots, *...  26.6 us
    unnamed x62, local copies, waits for them, and re-layouts  21.7 us
    pallas_call x2, Pallas kernels, sum_over(): pl.pallas_call(lambda *refs: sum_kernel(axes, sizes, *refs), out_shape=ja...  21 us
    unnamed x4, other arithmetic  18.7 us
  transfers between devices with their start and end apart: 17, of which 11 were waited for; matrix products, arithmetic and copies ran while one was open for 8% of the time, Pallas kernels for 0%

profile of v3, /device:TPU:0, one launch (start us, length us, event | category | flops | bytes accessed | tf_op | source)
XLA Modules:
  0.0 450.9 jit_solution(5857935447821913341)
XLA Ops:
  0.7 1.0 select_reduce_fusion.1
  2.7 1.9 convert_reduce_fusion
  4.6 1.7 convert_reduce_fusion.1
  6.8 26.6 %shard_map.282 = (f32[8,200,3200]{2,1,0:T(8,128)}, f32[8,16,128]{2,1,0:T(8,128)S(1)}) custom-call(s32[128]{0:T(128)S(1)} %select_reduce_fusion.refs_0_, s32[128]{0:T(128)S(1)} %convert_element_type.109.refs_1_, bf16[10,200,512]{2,1,0:T(8,128)(2,1)S(1)} %pad_maximum_fusion.1.refs_2_, bf16[14,200,512]{2,1,0:T(8,128)(2,1)S(1)} %pad_maximum_fusion.refs_3_), custom_call_target="tpu_custom_call" | custom-call | tf_op jit(solution)/shard_map/pallas_call | solution.py:63
  34.2 10.2 %shard_map.283 = f32[8,384]{1,0:T(8,128)} custom-call(f32[8,384]{1,0:T(8,128)} %reshape.163.refs_0_), custom_call_target="tpu_custom_call" | custom-call | tf_op jit(solution)/shard_map/pallas_call | solution.py:154
  45.8 6.3 %fusion.21 = (f16[200,3200]{1,0:T(8,128)(2,1)}, f16[200,3200]{1,0:T(8,128)(2,1)}, f16[200,3200]{1,0:T(8,128)(2,1)}, f16[200,3200]{1,0:T(8,128)(2,1)S(1)}) fusion(f32[8,200,3200]{2,1,0:T(8,128)} %get-tuple-element.15, s32[]{:T(128)S(6)} %select_n.259, f32[3200]{0:T(1024)S(1)} %get-tuple-element.57, f32[3200]{0:T(1024)S(1)} %get-tuple-element.58, ...), kind=kLoop, calls=%fused_computation.38 | loop fusion | flops 5120000 | bytes 15411216 | tf_op jit(solution)/shard_map/convert_element_type | solution.py:272
  52.1 1.6 collective-permute-start
  53.7 27.4 %collective-permute-done = f16[200,3200]{1,0:T(8,128)(2,1)S(1)} collective-permute-done((f16[200,3200]{1,0:T(8,128)(2,1)S(1)}, f16[200,3200]{1,0:T(8,128)(2,1)S(1)}, u32[]{:S(2)}, u32[]{:S(2)}) %collective-permute-start) | collective-permute-done | bytes 1280032 | tf_op jit(solution)/shard_map/ppermute | solution.py:273
  81.1 2.1 fusion.35
  83.2 1.0 collective-permute-start.1
  84.2 1.3 collective-permute-start.2
  85.5 27.6 %collective-permute-done.1 = f16[200,3200]{1,0:T(8,128)(2,1)S(1)} collective-permute-done((f16[200,3200]{1,0:T(8,128)(2,1)S(1)}, f16[200,3200]{1,0:T(8,128)(2,1)S(1)}, u32[]{:S(2)}, u32[]{:S(2)}) %collective-permute-start.1) | collective-permute-done | bytes 1280032 | tf_op jit(solution)/shard_map/ppermute | solution.py:283
  113.2 1.0 copy-done.19
  115.4 2.5 fusion.32
  117.9 1.1 collective-permute-start.3
  119.0 1.6 collective-permute-start.4
  120.6 24.5 %collective-permute-done.3 = f16[200,3200]{1,0:T(8,128)(2,1)S(1)} collective-permute-done((f16[200,3200]{1,0:T(8,128)(2,1)S(1)}, f16[200,3200]{1,0:T(8,128)(2,1)S(1)}, u32[]{:S(2)}, u32[]{:S(2)}) %collective-permute-start.3) | collective-permute-done | bytes 1280032 | tf_op jit(solution)/shard_map/ppermute | solution.py:283
  145.1 1.0 copy-done.20
  147.4 3.5 fusion.29
  151.2 1.1 collective-permute-start.6
  153.4 52.5 %collective-permute-done.5 = f16[200,3200]{1,0:T(8,128)(2,1)} collective-permute-done((f16[200,3200]{1,0:T(8,128)(2,1)}, f16[200,3200]{1,0:T(8,128)(2,1)}, u32[]{:S(2)}, u32[]{:S(2)}) %collective-permute-start.5) | collective-permute-done | bytes 1280032 | tf_op jit(solution)/shard_map/ppermute | solution.py:283
  205.8 1.1 slice.65
  207.7 5.6 %fusion.26 = f32[200,3200]{1,0:T(8,128)} fusion(f16[200,3200]{1,0:T(8,128)(2,1)} %collective-permute-done.5, f16[200,3200]{1,0:T(8,128)(2,1)} %copy-done.20, f16[200,3200]{1,0:T(8,128)(2,1)} %copy-done.19, f16[200,3200]{1,0:T(8,128)(2,1)} %collective-permute-done.6, f32[8,200,3200]{2,1,0:T(8,128)} %get-tuple-element.15, s32[]{:T(128)S(6)} %select_n.257, ...), kind=kLoop, calls=%fused_computation.44 | loop fusion | flops 6400000 | bytes 10265604 | tf_op jit(solution)/shard_map/mul | solution.py:288
  213.2 6.9 %reshape.164 = f32[200,16,200]{2,1,0:T(8,128)} reshape(f32[200,3200]{1,0:T(8,128)} %fusion.26) | data formatting | bytes 5120000 | tf_op jit(solution)/shard_map/reshape | solution.py:289
  220.2 8.6 %fusion.8 = f32[16,200,200]{1,2,0:T(8,128)S(1)} fusion(f32[1,16,200,200]{3,2,1,0:T(8,128)} %param.30, f32[200,16,200]{2,1,0:T(8,128)} %reshape.164, pred[16]{0:T(512)(128)(4,1)S(1)} %dynamic_slice.59), kind=kOutput, calls=%fused_computation.16 | convolution fusion | flops 1536640000 | bytes 7680016 | tf_op jit(solution)/shard_map/sij,sjk->sik/dot_general | solution.py:298
  228.8 5.2 %multiply_reduce_fusion = (f32[16]{0:T(128)S(1)}, f32[16,200,200]{2,1,0:T(8,128)}) fusion(f32[16,200,200]{1,2,0:T(8,128)S(1)} %fusion.8, f32[1,16,200,200]{3,2,1,0:T(8,128)S(1)} %copy-done), kind=kOutput, calls=%fused_computation.33 | convolution fusion | flops 1537280000 | bytes 7680064 | tf_op jit(solution)/shard_map/sij,sjk->sik/dot_general | solution.py:299
  234.0 5.6 %fusion.5 = (f32[1,16,200,200]{3,2,1,0:T(8,128)}, f32[16]{0:T(128)S(1)}) fusion(f32[1,16,200,200]{3,2,1,0:T(8,128)S(1)} %copy-done.13, f32[200,16,200]{2,1,0:T(8,128)S(1)} %copy-done.4, pred[16]{0:T(512)(128)(4,1)S(1)} %dynamic_slice.59, f32[]{:T(128)} %bitcast.27), kind=kLoop, calls=%fused_computation.13 | loop fusion | flops 7039984 | bytes 7680084 | tf_op jit(solution)/shard_map/broadcast_in_dim | solution.py:383
  241.0 2.5 select_select_fusion.3.refs_0_
  243.5 10.8 %shard_map.284 = f32[8,128]{1,0:T(8,128)} custom-call(f32[8,128]{1,0:T(8,128)} %select_select_fusion.3.refs_0_), custom_call_target="tpu_custom_call" | custom-call | tf_op jit(solution)/shard_map/pallas_call | solution.py:154
  254.3 0.8 fusion.49
  255.8 1.3 broadcast_select_fusion
  257.1 6.8 %constant_dynamic-update-slice_fusion.7 = (bf16[128,200,200]{2,1,0:T(8,128)(2,1)}, bf16[16,200,200]{2,1,0:T(8,128)(2,1)}, f32[16,200,200]{2,1,0:T(8,128)}) fusion(f32[16,200,200]{2,1,0:T(8,128)S(1)} %copy-done.6, f32[16]{0:T(128)S(1)} %broadcast_select_fusion, f32[1,16,200,200]{3,2,1,0:T(8,128)} %param.26, f32[1,16,200,200]{3,2,1,0:T(8,128)} %param.25, ...), kind=kLoop, calls=%fused_computation.86 | loop fusion | flops 6399999 | bytes 14233680
  263.9 0.8 collective-permute-start.7
  264.7 3.7 collective-permute-start.8
  268.4 1.3 collective-permute-start.9
  269.7 31.3 %collective-permute-done.7 = bf16[16,200,200]{2,1,0:T(8,128)(2,1)S(1)} collective-permute-done((bf16[16,200,200]{2,1,0:T(8,128)(2,1)}, bf16[16,200,200]{2,1,0:T(8,128)(2,1)S(1)}, u32[]{:S(2)}, u32[]{:S(2)}) %collective-permute-start.7) | collective-permute-done | bytes 1280032 | tf_op jit(solution)/shard_map/ppermute | solution.py:344
  302.9 4.0 collective-permute-done.9
  306.9 3.8 constant_dynamic-update-slice_fusion.6
  310.7 1.2 collective-permute-start.10
  311.9 2.7 collective-permute-start.11
  314.6 1.3 collective-permute-start.12
  315.9 30.3 %collective-permute-done.10 = bf16[16,200,200]{2,1,0:T(8,128)(2,1)S(1)} collective-permute-done((bf16[16,200,200]{2,1,0:T(8,128)(2,1)S(1)}, bf16[16,200,200]{2,1,0:T(8,128)(2,1)S(1)}, u32[]{:S(2)}, u32[]{:S(2)}) %collective-permute-start.10) | collective-permute-done | bytes 1280032 | tf_op jit(solution)/shard_map/ppermute | solution.py:355
  348.1 3.6 collective-permute-done.12
  351.7 4.5 constant_dynamic-update-slice_fusion.5
  356.9 2.8 collective-permute-start.14
  359.7 1.3 collective-permute-start.15
  362.4 12.8 %fusion.2 = f32[1,16,200,200]{3,2,1,0:T(8,128)} fusion(f32[1,16,200,200]{3,2,1,0:T(8,128)} %param.29, f32[200,16,200]{2,1,0:T(8,128)S(1)} %copy-done.5, pred[16]{0:T(512)(128)(4,1)S(1)} %dynamic_slice.59), kind=kOutput, calls=%fused_computation.6 | convolution fusion | flops 1539200000 | bytes 7680016 | tf_op jit(solution)/shard_map/ski,skj->sij/dot_general | solution.py:321
  375.2 15.4 %collective-permute-done.13 = bf16[16,200,200]{2,1,0:T(8,128)(2,1)} collective-permute-done((bf16[16,200,200]{2,1,0:T(8,128)(2,1)}, bf16[16,200,200]{2,1,0:T(8,128)(2,1)}, u32[]{:S(2)}, u32[]{:S(2)}) %collective-permute-start.13) | collective-permute-done | bytes 1280032 | tf_op jit(solution)/shard_map/ppermute | solution.py:355
  390.6 1.2 slice.68
  393.1 2.2 collective-permute-done.15
  395.3 3.6 constant_dynamic-update-slice_fusion.4
  398.9 1.4 collective-permute-start.16
  400.3 2.3 fusion.17
  402.7 9.4 %fusion.4 = f32[1,16,200,200]{3,2,1,0:T(8,128)} fusion(f32[1,16,200,200]{3,2,1,0:T(8,128)S(1)} %copy-done.12, f32[200,16,200]{2,1,0:T(8,128)S(1)} %copy-done.5, pred[16]{0:T(512)(128)(4,1)S(1)} %dynamic_slice.59), kind=kOutput, calls=%fused_computation.10 | convolution fusion | flops 1539200000 | bytes 7680016 | tf_op jit(solution)/shard_map/sik,sjk->sij/dot_general | solution.py:318
  412.0 1.3 constant_dynamic-update-slice_fusion.3
  414.1 1.4 constant_dynamic-update-slice_fusion.2
  415.4 2.7 constant_dynamic-update-slice_fusion.1
  418.1 13.3 %collective-permute-done.16 = bf16[16,200,200]{2,1,0:T(8,128)(2,1)S(1)} collective-permute-done((bf16[16,200,200]{2,1,0:T(8,128)(2,1)S(1)}, bf16[16,200,200]{2,1,0:T(8,128)(2,1)S(1)}, u32[]{:S(2)}, u32[]{:S(2)}) %collective-permute-start.16) | collective-permute-done | bytes 1280032 | tf_op jit(solution)/shard_map/ppermute | solution.py:355
  431.4 1.3 constant_dynamic-update-slice_fusion.refs_1_.refs_2_.refs_3_.refs_4_.refs_5_.refs_6_.refs_7_.refs_8_
  432.8 4.7 %copy-done.2 = bf16[128,200,200]{2,1,0:T(8,128)(2,1)S(1)} copy-done((bf16[128,200,200]{2,1,0:T(8,128)(2,1)S(1)}, bf16[128,200,200]{2,1,0:T(8,128)(2,1)}, u32[]{:S(2)}) %copy-start.2) | copy-done | bytes 10240024
  437.5 2.3 shard_map.285
  439.8 1.9 copy-done.3
  441.7 2.0 shard_map.286
  443.7 6.7 %copy.41 = bf16[1600,1200]{0,1:T(8,128)(2,1)} copy(bf16[1600,1200]{1,0:T(8,128)(2,1)} %copy-done.3) | data formatting | bytes 7680000
  (94 shorter events, 11.1 us)
Async XLA Ops:
  0.6 228.1 %copy-start = (f32[1,16,200,200]{3,2,1,0:T(8,128)S(1)}, f32[1,16,200,200]{3,2,1,0:T(8,128)}, u32[]{:S(2)}) copy-start(f32[1,16,200,200]{3,2,1,0:T(8,128)} %param.31) | copy-start | bytes 7680004
  2.6 3.6 copy-start.9
  2.7 3.6 copy-start.11
  4.6 2.0 copy-start.18
  4.6 2.0 copy-start.21
  52.1 29.0 %collective-permute-start = (f16[200,3200]{1,0:T(8,128)(2,1)S(1)}, f16[200,3200]{1,0:T(8,128)(2,1)S(1)}, u32[]{:S(2)}, u32[]{:S(2)}) collective-permute-start(f16[200,3200]{1,0:T(8,128)(2,1)S(1)} %get-tuple-element.89), channel_id=1, source_target_pairs={{0,4},{4,0},{8,12},{12,8},{16,20},{20,16},{24,28},{28,24},{1,5},{5... | collective-permute-start | bytes 3840008 | tf_op jit(solution)/shard_map/ppermute | solution.py:273
  83.2 29.9 %collective-permute-start.1 = (f16[200,3200]{1,0:T(8,128)(2,1)S(1)}, f16[200,3200]{1,0:T(8,128)(2,1)S(1)}, u32[]{:S(2)}, u32[]{:S(2)}) collective-permute-start(f16[200,3200]{1,0:T(8,128)(2,1)S(1)} %fusion.35), channel_id=1, source_target_pairs={{0,8},{4,12},{8,16},{12,20},{16,24},{20,28},{24,0},{28,4},{1,9},{5... | collective-permute-start | bytes 3840008 | tf_op jit(solution)/shard_map/ppermute | solution.py:283
  84.2 31.2 %collective-permute-start.2 = (f16[200,3200]{1,0:T(8,128)(2,1)}, f16[200,3200]{1,0:T(8,128)(2,1)}, u32[]{:S(2)}, u32[]{:S(2)}) collective-permute-start(f16[200,3200]{1,0:T(8,128)(2,1)} %get-tuple-element.88), channel_id=1, source_target_pairs={{0,4},{4,0},{8,12},{12,8},{16,20},{20,16},{24,28},{28,24},{1,5},{5... | collective-permute-start | bytes 3840008 | tf_op jit(solution)/shard_map/ppermute | solution.py:273
  113.2 1.0 copy-start.19
  117.9 27.2 %collective-permute-start.3 = (f16[200,3200]{1,0:T(8,128)(2,1)S(1)}, f16[200,3200]{1,0:T(8,128)(2,1)S(1)}, u32[]{:S(2)}, u32[]{:S(2)}) collective-permute-start(f16[200,3200]{1,0:T(8,128)(2,1)S(1)} %fusion.32), channel_id=1, source_target_pairs={{0,24},{4,28},{8,0},{12,4},{16,8},{20,12},{24,16},{28,20},{1,25},{... | collective-permute-start | bytes 3840008 | tf_op jit(solution)/shard_map/ppermute | solution.py:283
  119.0 28.3 %collective-permute-start.4 = (f16[200,3200]{1,0:T(8,128)(2,1)}, f16[200,3200]{1,0:T(8,128)(2,1)}, u32[]{:S(2)}, u32[]{:S(2)}) collective-permute-start(f16[200,3200]{1,0:T(8,128)(2,1)} %get-tuple-element.87), channel_id=1, source_target_pairs={{0,4},{4,0},{8,12},{12,8},{16,20},{20,16},{24,28},{28,24},{1,5},{5... | collective-permute-start | bytes 3840008 | tf_op jit(solution)/shard_map/ppermute | solution.py:273
  145.1 1.0 copy-start.20
  150.9 54.9 %collective-permute-start.5 = (f16[200,3200]{1,0:T(8,128)(2,1)}, f16[200,3200]{1,0:T(8,128)(2,1)}, u32[]{:S(2)}, u32[]{:S(2)}) collective-permute-start(f16[200,3200]{1,0:T(8,128)(2,1)} %fusion.29), channel_id=1, source_target_pairs={{0,16},{4,20},{8,24},{12,28},{16,0},{20,4},{24,8},{28,12},{1,17},{... | collective-permute-start | bytes 3840008 | tf_op jit(solution)/shard_map/ppermute | solution.py:283
  151.2 56.4 %collective-permute-start.6 = (f16[200,3200]{1,0:T(8,128)(2,1)}, f16[200,3200]{1,0:T(8,128)(2,1)}, u32[]{:S(2)}, u32[]{:S(2)}) collective-permute-start(f16[200,3200]{1,0:T(8,128)(2,1)} %get-tuple-element.86), channel_id=1, source_target_pairs={{0,4},{4,0},{8,12},{12,8},{16,20},{20,16},{24,28},{28,24},{1,5},{5... | collective-permute-start | bytes 3840008 | tf_op jit(solution)/shard_map/ppermute | solution.py:273
  228.7 5.2 %copy-start.4 = (f32[200,16,200]{2,1,0:T(8,128)S(1)}, f32[200,16,200]{2,1,0:T(8,128)}, u32[]{:S(2)}) copy-start(f32[200,16,200]{2,1,0:T(8,128)} %reshape.164) | copy-start | bytes 7680004
  228.7 5.2 %copy-start.13 = (f32[1,16,200,200]{3,2,1,0:T(8,128)S(1)}, f32[1,16,200,200]{3,2,1,0:T(8,128)}, u32[]{:S(2)}) copy-start(f32[1,16,200,200]{3,2,1,0:T(8,128)} %param.27) | copy-start | bytes 7680004
  234.0 23.1 %copy-start.6 = (f32[16,200,200]{2,1,0:T(8,128)S(1)}, f32[16,200,200]{2,1,0:T(8,128)}, u32[]{:S(2)}) copy-start(f32[16,200,200]{2,1,0:T(8,128)} %get-tuple-element.99) | copy-start | bytes 7680004
  263.9 37.2 %collective-permute-start.7 = (bf16[16,200,200]{2,1,0:T(8,128)(2,1)}, bf16[16,200,200]{2,1,0:T(8,128)(2,1)S(1)}, u32[]{:S(2)}, u32[]{:S(2)}) collective-permute-start(bf16[16,200,200]{2,1,0:T(8,128)(2,1)} %get-tuple-element.83), channel_id=1, source_target_pairs={{0,4},{4,0},{8,12},{12,8},{16,20},{20,16},{24,28},{28,24},{1,5},{5... | collective-permute-start | bytes 3840008 | tf_op jit(solution)/shard_map/ppermute | solution.py:344
  264.7 38.2 %collective-permute-start.8 = (bf16[16,200,200]{2,1,0:T(8,128)(2,1)}, bf16[16,200,200]{2,1,0:T(8,128)(2,1)}, u32[]{:S(2)}, u32[]{:S(2)}) collective-permute-start(bf16[16,200,200]{2,1,0:T(8,128)(2,1)} %get-tuple-element.83), channel_id=1, source_target_pairs={{0,8},{4,12},{8,16},{12,20},{16,24},{20,28},{1,9},{5,13},{9,17},{1... | collective-permute-start | bytes 3840008 | tf_op jit(solution)/shard_map/ppermute | solution.py:337
  268.4 38.5 %collective-permute-start.9 = (bf16[16,200,200]{2,1,0:T(8,128)(2,1)}, bf16[16,200,200]{2,1,0:T(8,128)(2,1)S(1)}, u32[]{:S(2)}, u32[]{:S(2)}) collective-permute-start(bf16[16,200,200]{2,1,0:T(8,128)(2,1)} %get-tuple-element.83), channel_id=1, source_target_pairs={{8,0},{12,4},{16,8},{20,12},{24,16},{28,20},{9,1},{13,5},{17,9},{2... | collective-permute-start | bytes 3840008 | tf_op jit(solution)/shard_map/ppermute | solution.py:338
  301.1 9.6 %copy-start.14 = (bf16[16,200,200]{2,1,0:T(8,128)(2,1)}, bf16[16,200,200]{2,1,0:T(8,128)(2,1)S(1)}, u32[]{:S(2)}) copy-start(bf16[16,200,200]{2,1,0:T(8,128)(2,1)S(1)} %collective-permute-done.7) | copy-start | bytes 3840004
  306.9 7.7 %copy-start.10 = (bf16[16,200,200]{2,1,0:T(8,128)(2,1)}, bf16[16,200,200]{2,1,0:T(8,128)(2,1)S(1)}, u32[]{:S(2)}) copy-start(bf16[16,200,200]{2,1,0:T(8,128)(2,1)S(1)} %collective-permute-done.9) | copy-start | bytes 3840004
  310.7 35.5 %collective-permute-start.10 = (bf16[16,200,200]{2,1,0:T(8,128)(2,1)S(1)}, bf16[16,200,200]{2,1,0:T(8,128)(2,1)S(1)}, u32[]{:S(2)}, u32[]{:S(2)}) collective-permute-start(bf16[16,200,200]{2,1,0:T(8,128)(2,1)S(1)} %get-tuple-element.81), channel_id=1, source_target_pairs={{0,4},{4,0},{8,12},{12,8},{16,20},{20,16},{24,28},{28,24},{1,5},{5... | collective-permute-start | bytes 3840008 | tf_op jit(solution)/shard_map/ppermute | solution.py:355
  311.9 36.1 %collective-permute-start.11 = (bf16[16,200,200]{2,1,0:T(8,128)(2,1)}, bf16[16,200,200]{2,1,0:T(8,128)(2,1)}, u32[]{:S(2)}, u32[]{:S(2)}) collective-permute-start(bf16[16,200,200]{2,1,0:T(8,128)(2,1)} %collective-permute-done.8), channel_id=1, source_target_pairs={{0,8},{4,12},{8,16},{12,20},{16,24},{20,28},{1,9},{5,13},{9,17},{1... | collective-permute-start | bytes 3840008 | tf_op jit(solution)/shard_map/ppermute | solution.py:337
  314.6 37.0 %collective-permute-start.12 = (bf16[16,200,200]{2,1,0:T(8,128)(2,1)S(1)}, bf16[16,200,200]{2,1,0:T(8,128)(2,1)}, u32[]{:S(2)}, u32[]{:S(2)}) collective-permute-start(bf16[16,200,200]{2,1,0:T(8,128)(2,1)S(1)} %collective-permute-done.9), channel_id=1, source_target_pairs={{8,0},{12,4},{16,8},{20,12},{24,16},{28,20},{9,1},{13,5},{17,9},{2... | collective-permute-start | bytes 3840008 | tf_op jit(solution)/shard_map/ppermute | solution.py:338
  346.2 5.5 %copy-start.16 = (bf16[16,200,200]{2,1,0:T(8,128)(2,1)}, bf16[16,200,200]{2,1,0:T(8,128)(2,1)S(1)}, u32[]{:S(2)}) copy-start(bf16[16,200,200]{2,1,0:T(8,128)(2,1)S(1)} %collective-permute-done.10) | copy-start | bytes 3840004
  351.6 9.3 %copy-start.22 = (f32[8,384]{1,0:T(8,128)S(1)}, f32[8,384]{1,0:T(8,128)}, u32[]{:S(2)}) copy-start(f32[8,384]{1,0:T(8,128)} %shard_map.283) | copy-start | bytes 36868
  351.7 9.4 %copy-start.23 = (f32[1600]{0:T(1024)S(1)}, f32[1600]{0:T(1024)}, u32[]{:S(2)}) copy-start(f32[1600]{0:T(1024)} %param.35) | copy-start | bytes 19204
  351.7 9.4 %copy-start.24 = (f32[1600]{0:T(1024)S(1)}, f32[1600]{0:T(1024)}, u32[]{:S(2)}) copy-start(f32[1600]{0:T(1024)} %param.36) | copy-start | bytes 19204
  351.7 9.4 %copy-start.25 = (f32[1600]{0:T(1024)S(1)}, f32[1600]{0:T(1024)}, u32[]{:S(2)}) copy-start(f32[1600]{0:T(1024)} %param.37) | copy-start | bytes 19204
  351.7 10.1 %copy-start.26 = (f32[1200]{0:T(1024)S(1)}, f32[1200]{0:T(1024)}, u32[]{:S(2)}) copy-start(f32[1200]{0:T(1024)} %param.32) | copy-start | bytes 14404
  351.7 10.1 %copy-start.27 = (f32[1200]{0:T(1024)S(1)}, f32[1200]{0:T(1024)}, u32[]{:S(2)}) copy-start(f32[1200]{0:T(1024)} %param.33) | copy-start | bytes 14404
  351.7 10.1 %copy-start.28 = (f32[1200]{0:T(1024)S(1)}, f32[1200]{0:T(1024)}, u32[]{:S(2)}) copy-start(f32[1200]{0:T(1024)} %param.34) | copy-start | bytes 14404
  351.7 10.7 %copy-start.5 = (f32[200,16,200]{2,1,0:T(8,128)S(1)}, f32[200,16,200]{2,1,0:T(8,128)}, u32[]{:S(2)}) copy-start(f32[200,16,200]{2,1,0:T(8,128)} %reshape.164) | copy-start | bytes 7680004
  356.2 34.4 %collective-permute-start.13 = (bf16[16,200,200]{2,1,0:T(8,128)(2,1)}, bf16[16,200,200]{2,1,0:T(8,128)(2,1)}, u32[]{:S(2)}, u32[]{:S(2)}) collective-permute-start(bf16[16,200,200]{2,1,0:T(8,128)(2,1)} %get-tuple-element.79), channel_id=1, source_target_pairs={{0,4},{4,0},{8,12},{12,8},{16,20},{20,16},{24,28},{28,24},{1,5},{5... | collective-permute-start | bytes 3840008 | tf_op jit(solution)/shard_map/ppermute | solution.py:355
  356.9 36.2 %collective-permute-start.14 = (bf16[16,200,200]{2,1,0:T(8,128)(2,1)}, bf16[16,200,200]{2,1,0:T(8,128)(2,1)}, u32[]{:S(2)}, u32[]{:S(2)}) collective-permute-start(bf16[16,200,200]{2,1,0:T(8,128)(2,1)} %collective-permute-done.11), channel_id=1, source_target_pairs={{0,8},{4,12},{8,16},{12,20},{16,24},{20,28},{1,9},{5,13},{9,17},{1... | collective-permute-start | bytes 3840008 | tf_op jit(solution)/shard_map/ppermute | solution.py:337
  359.7 35.6 %collective-permute-start.15 = (bf16[16,200,200]{2,1,0:T(8,128)(2,1)}, bf16[16,200,200]{2,1,0:T(8,128)(2,1)}, u32[]{:S(2)}, u32[]{:S(2)}) collective-permute-start(bf16[16,200,200]{2,1,0:T(8,128)(2,1)} %collective-permute-done.12), channel_id=1, source_target_pairs={{8,0},{12,4},{16,8},{20,12},{24,16},{28,20},{9,1},{13,5},{17,9},{2... | collective-permute-start | bytes 3840008 | tf_op jit(solution)/shard_map/ppermute | solution.py:338
  395.3 5.0 %copy-start.7 = (f32[16,200,200]{2,1,0:T(8,128)S(1)}, f32[16,200,200]{2,1,0:T(8,128)}, u32[]{:S(2)}) copy-start(f32[16,200,200]{2,1,0:T(8,128)} %get-tuple-element.99) | copy-start | bytes 7680004
  395.3 5.0 %copy-start.8 = (f32[1,16,200,200]{3,2,1,0:T(8,128)S(1)}, f32[1,16,200,200]{3,2,1,0:T(8,128)}, u32[]{:S(2)}) copy-start(f32[1,16,200,200]{3,2,1,0:T(8,128)} %param.26) | copy-start | bytes 7680004
  398.9 3.7 copy-start.12
  398.9 32.5 %collective-permute-start.16 = (bf16[16,200,200]{2,1,0:T(8,128)(2,1)S(1)}, bf16[16,200,200]{2,1,0:T(8,128)(2,1)S(1)}, u32[]{:S(2)}, u32[]{:S(2)}) collective-permute-start(bf16[16,200,200]{2,1,0:T(8,128)(2,1)S(1)} %get-tuple-element.77), channel_id=1, source_target_pairs={{0,4},{4,0},{8,12},{12,8},{16,20},{20,16},{24,28},{28,24},{1,5},{5... | collective-permute-start | bytes 3840008 | tf_op jit(solution)/shard_map/ppermute | solution.py:355
  402.7 9.4 %copy-start.15 = (bf16[16,200,200]{2,1,0:T(8,128)(2,1)S(1)}, bf16[16,200,200]{2,1,0:T(8,128)(2,1)}, u32[]{:S(2)}) copy-start(bf16[16,200,200]{2,1,0:T(8,128)(2,1)} %copy-done.14) | copy-start | bytes 3840004
  412.0 2.0 copy-start.17
  432.7 4.7 %copy-start.2 = (bf16[128,200,200]{2,1,0:T(8,128)(2,1)S(1)}, bf16[128,200,200]{2,1,0:T(8,128)(2,1)}, u32[]{:S(2)}) copy-start(bf16[128,200,200]{2,1,0:T(8,128)(2,1)} %constant_dynamic-update-slice_fusion.refs_1_.refs_2_.refs_3_.refs_4_.refs_5_.refs_6_.refs_7_.refs_8_) | copy-start | bytes 30720004
  439.8 1.9 copy-start.3
  441.7 8.7 %copy-start.1 = (f32[1,16,200,200]{3,2,1,0:T(8,128)S(1)}, f32[1,16,200,200]{3,2,1,0:T(8,128)}, u32[]{:S(2)}) copy-start(f32[1,16,200,200]{3,2,1,0:T(8,128)} %param.31) | copy-start | bytes 7680004
